TPU v7x, 32 devices: a whole 2x2x4 slice. The times are simulated.
32 devices in a mesh: gx: 8 (over z, x), gy: 4 (over y, core).
Axes of the slice: x: 2, y: 2, z: 4, core: 2. Of those that a mesh axis runs over, the one named last changes fastest.
Arguments:
- adjoint_block: float32 [4, 3, 64, 32, 512], P(None, None, None, 'gx', 'gy'), may hold values from -18 to 18
- base_flow: float32 [2, 3, 64, 32, 512], P(None, None, None, 'gx', 'gy'), may hold values from -4 to 4
- direct_modes: float32 [8, 3, 64, 32, 512], P(None, None, None, 'gx', 'gy'), may hold values from -0.0034179688 to 0.0034179688
- dual_modes: float32 [8, 3, 64, 32, 512], P(None, None, None, 'gx', 'gy'), may hold values from -0.6 to 0.6
Outputs:
- next_block: float32 [4, 3, 64, 32, 512], P(None, None, None, 'gx', 'gy')
- growth: float32 [4, 4], replicated
All inputs are finite; a program needn't handle non-finite values.
Results may differ from a plain program's by a relative error of at most 0.0001.
Values sent between devices are 32-bit elements; how exact they have to be, the bound alone decides.
No kernel may reach another device: no remote copies, remote signals or barrier semaphores. Data moves between devices by JAX's collectives and lax.ppermute only.
A program may use at most 128 MiB of HBM per device.

v0:
```python
import functools
import math

import jax
import jax.numpy as jnp
from jax import lax
from jax.experimental import pallas as pl
from jax.experimental.pallas import tpu as pltpu
from jax.sharding import PartitionSpec as P

step_size = 0.1
viscosity = 0.2
HALF = 0.5 * step_size
DIFF = step_size * viscosity
SUB = 8
LANES = 128


def lane_ids():
    return lax.broadcasted_iota(jnp.int32, (SUB, LANES), 1)


def row_ids():
    return lax.broadcasted_iota(jnp.int32, (SUB, LANES), 0)


def roll(x, shift, axis):
    shift %= x.shape[axis]
    return x if shift == 0 else pltpu.roll(x, shift, axis)


def block(ref, field, k):
    return ref[field, pl.ds(pl.multiple_of(k * SUB, SUB), SUB), :]


def put_block(ref, field, k, value):
    ref[field, pl.ds(pl.multiple_of(k * SUB, SUB), SUB), :] = value


def pairs_of(n):
    return [(i, j) for i in range(n) for j in range(i, n)]


def lane_sums(slots):
    half, lane = LANES // 2, lane_ids()
    while len(slots) > 1:
        count = len(slots) // 2
        low = (lane & half) == 0
        merged = []
        for one, two in zip(slots[:count], slots[count:]):
            if one is None and two is None:
                merged.append(None)
            elif two is None:
                merged.append(one + roll(one, -half, 1))
            elif one is None:
                merged.append(two + roll(two, half, 1))
            else:
                kept = jnp.where(low, one, two)
                moved = jnp.where(low, roll(one, -half, 1), roll(two, half, 1))
                merged.append(kept + moved)
        slots, half = merged, half // 2
    total = slots[0]
    while half >= 1:
        total = total + roll(total, half, 1)
        half //= 2
    for shift in (4, 2, 1):
        total = total + roll(total, shift, 0)
    return total


def spread(total, lane):
    return jnp.broadcast_to(total[:, lane : lane + 1], (SUB, LANES))


def gathered_total(ref):
    total = ref[0:SUB, :]
    for first in range(SUB, ref.shape[0], SUB):
        total = total + ref[first : first + SUB, :]
    for shift in (4, 2, 1):
        total = total + roll(total, shift, 0)
    return total


def call(kernel, outs, *args, scratch=(), vmem=None, any_args=()):
    specs = [
        pl.BlockSpec(memory_space=pl.ANY if i in any_args else pltpu.VMEM) for i in range(len(args))
    ]
    moved = sum(math.prod(a.shape) for a in args) + sum(math.prod(o) for o in outs)
    return pl.pallas_call(
        kernel,
        out_shape=[jax.ShapeDtypeStruct(shape, jnp.float32) for shape in outs],
        in_specs=specs,
        out_specs=[pl.BlockSpec(memory_space=pltpu.VMEM) for _ in outs],
        scratch_shapes=list(scratch),
        cost_estimate=pl.CostEstimate(flops=4 * moved, bytes_accessed=4 * moved, transcendentals=0),
    )(*args)


def pack_y(fields, left_ref, right_ref, blocks):
    lane = lane_ids()

    def step(k, carry):
        left = jnp.zeros((SUB, LANES), jnp.float32)
        right = left
        for n, (ref, f) in enumerate(fields):
            value = block(ref, f, k)
            left = jnp.where(lane == (2 * n - 1) % LANES, roll(value, 2 * n - 1, 1), left)
            right = jnp.where(lane == 2 * n, roll(value, 2 * n + 1, 1), right)
        rows = pl.ds(pl.multiple_of(k * SUB, SUB), SUB)
        left_ref[rows, :] = left
        right_ref[rows, :] = right
        return carry

    lax.fori_loop(0, blocks, step, 0)


def pack_x_kernel(width, groups, q_ref, base_ref, *outs):
    for (fields, first), (low, high) in zip(groups, zip(outs[::2], outs[1::2])):
        depth = low.shape[1]
        for n, (which, f) in enumerate(fields):
            ref = (q_ref, base_ref)[which]
            low[n] = ref[f, pl.ds(0, depth, stride=width), :]
            high[n] = ref[f, pl.ds(width - 1, depth, stride=width), :]


def pack_y_kernel(q_ref, base_ref, left_ref, right_ref):
    fields = [(q_ref, f) for f in range(q_ref.shape[0])]
    fields += [(base_ref, f) for f in range(base_ref.shape[0])]
    pack_y(fields, left_ref, right_ref, q_ref.shape[1] // SUB)


def modes_kernel(width, modes, slot, direct_ref, dual_ref, direct_planes, dual_planes, metric_ref):
    depth = direct_planes.shape[2]
    comps = direct_ref.shape[0] // modes
    for ref, planes in ((direct_ref, direct_planes), (dual_ref, dual_planes)):
        for f in range(ref.shape[0]):
            planes[0, f] = ref[f, pl.ds(0, depth, stride=width), :]
            planes[1, f] = ref[f, pl.ds(width - 1, depth, stride=width), :]
    todo = pairs_of(modes)
    slots = [None] * LANES
    for first in range(0, len(todo), 18):
        chunk = todo[first : first + 18]

        def step(k, accs):
            accs = list(accs)
            for c in range(comps):
                values = {m: block(dual_ref, m * comps + c, k) for m in set(sum(chunk, ()))}
                for n, (a, b) in enumerate(chunk):
                    accs[n] = accs[n] + values[a] * values[b]
            return tuple(accs)

        zero = jnp.zeros((SUB, LANES), jnp.float32)
        sums = lax.fori_loop(0, dual_ref.shape[1] // SUB, step, (zero,) * len(chunk))
        for n, value in enumerate(sums):
            slots[slot + first + n] = value
    lane = lane_ids()
    inside = (lane >= slot) & (lane < slot + len(todo))
    metric_ref[...] = jnp.where(inside, lane_sums(slots), 0.0)


def advance_kernel(width, width_comps, offset, y_offset, base_at, base_y, projections, others, *refs):
    comps = width_comps
    q_ref, base_ref, hq_l, hq_r, hb_l, hb_r = refs[:6]
    mode_refs = refs[6 : 6 + projections]
    other_refs = refs[6 + projections : 6 + projections + others]
    out_ref, planes_ref, sums_ref = refs[6 + projections + others :]
    fields, rows = out_ref.shape[:2]
    vectors, blocks = fields // comps, rows // SUB
    depth = rows // width
    lane, row = lane_ids(), row_ids()
    x_at = row % width
    low_x = jnp.where(x_at > 0, 1.0, 0.0)
    high_x = jnp.where(x_at < width - 1, 1.0, 0.0)
    upper = row < width

    def around(ref, f, k, before, after, halo, lane_at):
        here = block(ref, f, k)
        edge = roll(halo, -lane_at, 1)
        y_low = jnp.where(lane == 0, edge, roll(here, 1, 1))
        y_high = jnp.where(lane == LANES - 1, edge, roll(here, -1, 1))
        x_low, x_high = roll(here, 1, 0), roll(here, -1, 0)
        z_low, z_high = z_neighbours(here, block(ref, f, before), block(ref, f, after))
        return here, (x_low, y_low, z_low), (x_high, y_high, z_high)

    def z_neighbours(here, earlier, later):
        shift = SUB - width
        if shift == 0:
            return earlier, later
        low = roll(jnp.where(row < SUB - width, here, earlier), width, 0)
        high = roll(jnp.where(row < width, later, here), -width, 0)
        return low, high

    def step(k, carry):
        before = lax.rem(k + blocks - 1, blocks)
        after = lax.rem(k + 1, blocks)
        rows_k = pl.ds(pl.multiple_of(k * SUB, SUB), SUB)
        halo_q = hq_l[rows_k, :] + hq_r[rows_k, :]
        halo_b = hb_l[rows_k, :] + hb_r[rows_k, :]
        centre, grads = [], []
        for j in range(comps):
            here, low, high = around(base_ref, base_at + j, k, before, after, halo_b, 2 * (base_y + j))
            centre.append(HALF * here)
            grads.append(
                (
                    HALF * (high[0] * high_x - low[0] * low_x),
                    HALF * (high[1] - low[1]),
                    HALF * (high[2] - low[2]),
                )
            )
        plus = [(DIFF + centre[0]) * high_x, DIFF + centre[1], DIFF + centre[2]]
        minus = [(DIFF - centre[0]) * low_x, DIFF - centre[1], DIFF - centre[2]]
        for v in range(vectors):
            values = []
            sums = []
            for c in range(comps):
                f = v * comps + c
                here, low, high = around(
                    q_ref, offset + f, k, before, after, halo_q, 2 * (y_offset + f)
                )
                total = (1.0 - 6.0 * DIFF) * here
                for d in range(3):
                    total = total + plus[d] * high[d] + minus[d] * low[d]
                values.append(here)
                sums.append(total)
            for c in range(comps):
                total = sums[c]
                for j in range(comps):
                    total = total - values[j] * grads[j][c]
                put_block(out_ref, v * comps + c, k, total)
        return carry

    lax.fori_loop(0, blocks, step, 0)
    for f in range(fields):
        planes_ref[0, f] = out_ref[f, pl.ds(0, depth, stride=width), :]
        planes_ref[1, f] = out_ref[f, pl.ds(width - 1, depth, stride=width), :]

    zero = jnp.zeros((SUB, LANES), jnp.float32)
    at = 0
    for ref in mode_refs:
        modes = ref.shape[0] // comps

        def dots(k, accs):
            accs = list(accs)
            for c in range(comps):
                right = [block(out_ref, v * comps + c, k) for v in range(vectors)]
                for m in range(modes):
                    left = block(ref, m * comps + c, k)
                    for v in range(vectors):
                        accs[m * vectors + v] = accs[m * vectors + v] + left * right[v]
            return tuple(accs)

        for value in lax.fori_loop(0, blocks, dots, (zero,) * (modes * vectors)):
            sums_ref[at] = value
            at += 1
    if sums_ref.shape[0] > at:
        keep = (x_at > 0) & (x_at < width - 1)
        own = pairs_of(vectors)
        theirs = [(o, i, j) for o in range(others) for i in range(vectors) for j in range(vectors)]

        def gram(k, accs):
            accs = list(accs)
            for c in range(comps):
                inner = [jnp.where(keep, block(out_ref, v * comps + c, k), 0.0) for v in range(vectors)]
                for n, (i, j) in enumerate(own):
                    accs[n] = accs[n] + inner[i] * inner[j]
                for n, (o, i, j) in enumerate(theirs):
                    value = block(other_refs[o], i * comps + c, k)
                    accs[len(own) + n] = accs[len(own) + n] + value * inner[j]
            return tuple(accs)

        for value in lax.fori_loop(0, blocks, gram, (zero,) * (len(own) + len(theirs))):
            sums_ref[at] = value
            at += 1


def edge_kernel(comps, at, halo_base, lanes, others, extra, *refs):
    q_low, q_high, b_low, b_high, hq_low, hq_high, hb_low, hb_high, advanced, sums_ref = refs[:10]
    refs = refs[10:]
    modes_count = len(lanes)
    mode_refs, refs = refs[:modes_count], refs[modes_count:]
    other_refs, refs = refs[:others], refs[others:]
    extra_refs, refs = refs[:extra], refs[extra:]
    new_ref, payload_ref = refs
    q_at, base_at, hq_at, hb_at = at
    fields, depth = new_ref.shape[1:3]
    vectors, blocks = fields // comps, depth // SUB

    def delta(side, k):
        sign = (-1.0, 1.0)[side]
        own_q, own_b = (q_low, q_high)[side], (b_low, b_high)[side]
        halo_q, halo_b = (hq_low, hq_high)[side], (hb_low, hb_high)[side]
        factor = DIFF + (sign * HALF) * block(own_b, base_at, k)
        outer = [(sign * HALF) * block(halo_b, hb_at + j, k) for j in range(comps)]
        result = []
        for v in range(vectors):
            for c in range(comps):
                value = factor * block(halo_q, hq_at + v * comps + c, k)
                if c == 0:
                    for j in range(comps):
                        value = value - block(own_q, q_at + v * comps + j, k) * outer[j]
                result.append(value)
        return result

    at_sum = 0
    slots = {}
    for n, ref in enumerate(mode_refs):
        modes = ref.shape[1] // comps
        accs = tuple(sums_ref[at_sum + i] for i in range(modes * vectors))
        at_sum += modes * vectors
        for side in range(2):

            def step(k, accs, side=side, ref=ref, first=(n == 0)):
                accs = list(accs)
                changes = delta(side, k)
                for c in range(comps):
                    for m in range(modes):
                        left = ref[side, m * comps + c, pl.ds(pl.multiple_of(k * SUB, SUB), SUB), :]
                        for v in range(vectors):
                            accs[m * vectors + v] = accs[m * vectors + v] + left * changes[v * comps + c]
                if first:
                    rows = pl.ds(pl.multiple_of(k * SUB, SUB), SUB)
                    for f in range(fields):
                        new_ref[side, f, rows, :] = advanced[side, f, rows, :] + changes[f]
                return tuple(accs)

            accs = lax.fori_loop(0, blocks, step, accs)
        for i, value in enumerate(accs):
            slots[lanes[n][i]] = value
    if at_sum < sums_ref.shape[0]:
        own = pairs_of(vectors)
        theirs = [(o, i, j) for o in range(others) for i in range(vectors) for j in range(vectors)]
        accs = tuple(sums_ref[at_sum + i] for i in range(len(own) + len(theirs)))
        for side in range(2):

            def gram(k, accs, side=side):
                accs = list(accs)
                rows = pl.ds(pl.multiple_of(k * SUB, SUB), SUB)
                for c in range(comps):
                    inner = [new_ref[side, v * comps + c, rows, :] for v in range(vectors)]
                    for n, (i, j) in enumerate(own):
                        accs[n] = accs[n] + inner[i] * inner[j]
                    for n, (o, i, j) in enumerate(theirs):
                        value = other_refs[o][side, i * comps + c, rows, :]
                        accs[len(own) + n] = accs[len(own) + n] + value * inner[j]
                return tuple(accs)

            accs = lax.fori_loop(0, blocks, gram, accs)
        for i, value in enumerate(accs):
            slots[gram_lanes(lanes, i)] = value
    lane = lane_ids()
    inside = lane < 0
    for position in slots:
        inside = inside | (lane == position)
    total = jnp.where(inside, lane_sums([slots.get(i) for i in range(LANES)]), 0.0)
    for ref in extra_refs:
        total = total + ref[...]
    for first in range(0, payload_ref.shape[0], SUB):
        payload_ref[first : first + SUB, :] = total


def gram_lanes(lanes, i):
    return lanes.gram[i]


class Lanes(tuple):
    gram = ()


def deflate_planes_kernel(comps, lanes, gathered, planes, dual_planes, low_ref, high_ref, factors):
    total = gathered_total(gathered)
    for i, lane in enumerate(lanes):
        factors[i] = spread(total, lane)
    fields, depth = low_ref.shape[:2]
    vectors = fields // comps
    modes = dual_planes.shape[1] // comps
    for side, out in ((0, low_ref), (1, high_ref)):

        def step(k, carry, side=side, out=out):
            rows = pl.ds(pl.multiple_of(k * SUB, SUB), SUB)
            for c in range(comps):
                values = [planes[side, v * comps + c, rows, :] for v in range(vectors)]
                for m in range(modes):
                    mode = dual_planes[side, m * comps + c, rows, :]
                    for v in range(vectors):
                        values[v] = values[v] - factors[m * vectors + v] * mode
                for v in range(vectors):
                    out[v * comps + c, rows, :] = values[v]
            return carry

        lax.fori_loop(0, depth // SUB, step, 0)


def deflate_kernel(
    width, comps, lanes, gathered, advanced, dual, low_ref, high_ref, out_ref, left_ref, right_ref, factors
):
    total = gathered_total(gathered)
    for i, lane in enumerate(lanes):
        factors[i] = spread(total, lane)
    fields, rows_all = out_ref.shape[:2]
    vectors = fields // comps
    modes = dual.shape[0] // comps

    def step(k, carry):
        for c in range(comps):
            values = [block(advanced, v * comps + c, k) for v in range(vectors)]
            for m in range(modes):
                mode = block(dual, m * comps + c, k)
                for v in range(vectors):
                    values[v] = values[v] - factors[m * vectors + v] * mode
            for v in range(vectors):
                put_block(out_ref, v * comps + c, k, values[v])
        return carry

    lax.fori_loop(0, rows_all // SUB, step, 0)
    depth = rows_all // width
    for f in range(fields):
        out_ref[f, pl.ds(0, depth, stride=width), :] = low_ref[f]
        out_ref[f, pl.ds(width - 1, depth, stride=width), :] = high_ref[f]
    pack_y([(out_ref, f) for f in range(fields)], left_ref, right_ref, rows_all // SUB)


def finish_kernel(width, comps, layout, scale, groups, *refs):
    gathered, dual = refs[:2]
    advanced = refs[2 : 2 + groups]
    planes = refs[2 + groups : 2 + 2 * groups]
    out_ref, growth_ref, block_ref, factors, semaphore = refs[2 + 2 * groups :]
    fields, rows_all = out_ref.shape[:2]
    vectors, modes = fields // comps, dual.shape[0] // comps
    each = fields // groups
    copies = [
        pltpu.make_async_copy(advanced[g], block_ref.at[pl.ds(g * each, each)], semaphore.at[g])
        for g in range(groups)
    ]
    for copy in copies:
        copy.start()
    total = gathered_total(gathered)
    first, cross, self_gram, metric = layout
    coef = {key: spread(total, lane) for key, lane in first.items()}
    mixed = {key: spread(total, lane) for key, lane in cross.items()}
    inner = {key: spread(total, lane) for key, lane in self_gram.items()}
    weight = {key: spread(total, lane) for key, lane in metric.items()}
    weighted = {}
    for m in range(modes):
        for j in range(vectors):
            weighted[m, j] = sum(weight[min(m, n), max(m, n)] * coef[n, j] for n in range(modes))
    gram = {}
    for i, j in pairs_of(vectors):
        value = inner[i, j]
        for m in range(modes):
            value = value - coef[m, i] * (mixed[m, j] - weighted[m, j]) - coef[m, j] * mixed[m, i]
        gram[j, i] = value
    lower, inverse_diagonal = {}, {}
    for j in range(vectors):
        value = gram[j, j]
        for n in range(j):
            value = value - lower[j, n] * lower[j, n]
        lower[j, j] = jnp.sqrt(value)
        inverse_diagonal[j] = 1.0 / lower[j, j]
        for i in range(j + 1, vectors):
            value = gram[i, j]
            for n in range(j):
                value = value - lower[i, n] * lower[j, n]
            lower[i, j] = value * inverse_diagonal[j]
    inverse = {}
    for j in range(vectors):
        inverse[j, j] = inverse_diagonal[j]
        for i in range(j + 1, vectors):
            value = sum(lower[i, n] * inverse[n, j] for n in range(j, i))
            inverse[i, j] = -inverse_diagonal[i] * value
    row, lane = row_ids(), lane_ids()
    growth = jnp.zeros((SUB, LANES), jnp.float32)
    for (i, j), value in lower.items():
        growth = jnp.where((row == i) & (lane == j), value, growth)
    growth_ref[...] = growth[:vectors, :vectors]
    at = {}
    for (i, j), value in inverse.items():
        at[i, j] = len(at)
        factors[at[i, j]] = scale * value
    mode_at = {}
    for i in range(vectors):
        for m in range(modes):
            mode_at[i, m] = len(at) + len(mode_at)
            factors[mode_at[i, m]] = -scale * sum(inverse[i, j] * coef[m, j] for j in range(i + 1))
    for copy in copies:
        copy.wait()
    depth = rows_all // width
    for g in range(groups):
        for f in range(each):
            block_ref[g * each + f, pl.ds(0, depth, stride=width), :] = planes[g][0, f]
            block_ref[g * each + f, pl.ds(width - 1, depth, stride=width), :] = planes[g][1, f]

    def step(k, carry):
        for c in range(comps):
            parts = [block(block_ref, v * comps + c, k) for v in range(vectors)]
            values = []
            for i in range(vectors):
                value = factors[at[i, 0]] * parts[0]
                for j in range(1, i + 1):
                    value = value + factors[at[i, j]] * parts[j]
                values.append(value)
            for m in range(modes):
                mode = block(dual, m * comps + c, k)
                for i in range(vectors):
                    values[i] = values[i] + factors[mode_at[i, m]] * mode
            for i in range(vectors):
                put_block(out_ref, i * comps + c, k, values[i])
        return carry

    lax.fori_loop(0, rows_all // SUB, step, 0)


def shift(field, axis, up):
    count = lax.axis_size(axis)
    pairs = [(i, i + 1) for i in range(count - 1)]
    return lax.ppermute(field, axis, pairs if up else [(j, i) for i, j in pairs])


def halos(low, high, axis):
    return shift(high, axis, True), shift(low, axis, False)


def exchange(payload):
    return lax.all_to_all(payload, ("gx", "gy"), 0, 0, tiled=True)


def body(adjoint_block, base_flow, direct_modes, dual_modes):
    vectors, comps, depth, width, length = adjoint_block.shape
    steps, modes = base_flow.shape[0], direct_modes.shape[0]
    rows = depth * width
    assert length == LANES and SUB % width == 0 and rows % SUB == 0 and depth % SUB == 0
    devices = lax.axis_size("gx") * lax.axis_size("gy")
    cells = float(comps * rows * length * devices)
    groups = 2
    size = vectors // groups
    part = size * comps

    q = adjoint_block.reshape(vectors * comps, rows, length)
    base = base_flow.reshape(steps * comps, rows, length)
    direct = direct_modes.reshape(modes * comps, rows, length)
    dual = dual_modes.reshape(modes * comps, rows, length)

    plane = (depth, length)
    sets = []
    for g in range(groups):
        fields = [(0, g * part + f) for f in range(part)]
        if g == 0:
            fields += [(1, j) for j in range(comps)]
        sets.append((fields, None))
    sets.append(([(1, comps + j) for j in range(comps)], None))
    packed = call(
        functools.partial(pack_x_kernel, width, sets),
        [(len(fields), *plane) for fields, _ in sets for _ in range(2)],
        q,
        base,
    )
    lows, highs = packed[::2], packed[1::2]
    halo_x = [halos(low, high, "gx") for low, high in zip(lows, highs)]
    left, right = call(pack_y_kernel, [(rows, LANES)] * 2, q, base)
    halo_y = halos(left, right, "gy")

    pairs, mode_pairs = pairs_of(vectors), pairs_of(modes)
    first = {(m, i): m * vectors + i for m in range(modes) for i in range(vectors)}
    cross = {key: modes * vectors + lane for key, lane in first.items()}
    self_gram = {key: 2 * modes * vectors + n for n, key in enumerate(pairs)}
    slot = 2 * modes * vectors + len(pairs)
    metric = {key: slot + n for n, key in enumerate(mode_pairs)}
    assert slot + len(mode_pairs) <= LANES
    direct_planes, dual_planes, metric_part = call(
        functools.partial(modes_kernel, width, modes, slot),
        [(2, modes * comps, *plane)] * 2 + [(SUB, LANES)],
        direct,
        dual,
    )

    spacing = LANES // (1 << (modes * size - 1).bit_length())
    group_lanes = [spacing * n for n in range(modes * size)]
    advanced, gathered, edge = [], [], []
    for g in range(groups):
        kernel = functools.partial(advance_kernel, width, comps, g * part, g * part, 0, vectors * comps, 1, 0)
        out, planes, sums = call(
            kernel,
            [(part, rows, length), (2, part, *plane), (modes * size, SUB, LANES)],
            q,
            base,
            *halo_y,
            *halo_y,
            direct,
        )
        lanes = Lanes([group_lanes])
        new, payload = call(
            functools.partial(edge_kernel, comps, (0, part, 0, part), None, lanes, 0, 0),
            [(2, part, *plane), (devices, LANES)],
            lows[g],
            highs[g],
            lows[0],
            highs[0],
            *halo_x[g],
            *halo_x[0],
            planes,
            sums,
            direct_planes,
        )
        advanced.append(out)
        edge.append(new)
        gathered.append(exchange(payload))

    blocks, planes_new, parts = [], [], [metric_part]
    for g in range(groups):
        scratch = [pltpu.VMEM((modes * size, SUB, LANES), jnp.float32)]
        low, high = call(
            functools.partial(deflate_planes_kernel, comps, group_lanes),
            [(part, *plane)] * 2,
            gathered[g],
            edge[g],
            dual_planes,
            scratch=scratch,
        )
        outer_x = halos(low, high, "gx")
        current, left, right = call(
            functools.partial(deflate_kernel, width, comps, group_lanes),
            [(part, rows, length), (rows, LANES), (rows, LANES)],
            gathered[g],
            advanced[g],
            dual,
            low,
            high,
            scratch=scratch,
        )
        outer_y = halos(left, right, "gy")
        kernel = functools.partial(
            advance_kernel, width, comps, 0, 0, comps, vectors * comps + comps, 2, len(blocks)
        )
        grams = size * (size + 1) // 2 + len(blocks) * size * size
        out, planes, sums = call(
            kernel,
            [(part, rows, length), (2, part, *plane), (2 * modes * size + grams, SUB, LANES)],
            current,
            base,
            *outer_y,
            *halo_y,
            direct,
            dual,
            *blocks,
        )
        own = [g * size + i for i in range(size)]
        lanes = Lanes(
            [[table[m, i] for m in range(modes) for i in own] for table in (first, cross)]
        )
        lanes.gram = [self_gram[own[i], own[j]] for i, j in pairs_of(size)]
        lanes.gram += [self_gram[o * size + i, j] for o in range(len(blocks)) for i in range(size) for j in own]
        new, payload = call(
            functools.partial(
                edge_kernel, comps, (0, 0, 0, 0), None, lanes, len(blocks), len(parts) if g == groups - 1 else 0
            ),
            [(2, part, *plane), (devices if g == groups - 1 else SUB, LANES)],
            low,
            high,
            lows[groups],
            highs[groups],
            *outer_x,
            *halo_x[groups],
            planes,
            sums,
            direct_planes,
            dual_planes,
            *planes_new,
            *(parts if g == groups - 1 else ()),
        )
        blocks.append(out)
        planes_new.append(new)
        parts.append(payload)

    total = exchange(parts[-1])
    factor_count = vectors * (vectors + 1) // 2 + modes * vectors
    next_block, growth = call(
        functools.partial(
            finish_kernel, width, comps, (first, cross, self_gram, metric), math.sqrt(cells), groups
        ),
        [(vectors * comps, rows, length), (vectors, vectors)],
        total,
        dual,
        *blocks,
        *planes_new,
        scratch=[
            pltpu.VMEM((vectors * comps, rows, length), jnp.float32),
            pltpu.VMEM((factor_count, SUB, LANES), jnp.float32),
            pltpu.SemaphoreType.DMA((groups,)),
        ],
        any_args=tuple(range(2, 2 + groups)),
    )
    return (next_block.reshape(adjoint_block.shape), growth)


def solution(mesh):
    placed = P(None, None, None, "gx", "gy")
    return jax.shard_map(
        body,
        mesh=mesh,
        in_specs=(placed,) * 4,
        out_specs=(placed, P()),
        check_vma=False,
    )
```

profile of v0, /device:TPU:0, one launch (start us, length us, event | category | flops | bytes accessed | tf_op | source)
XLA Modules:
  0.0 172.2 jit_solution(2936413413076659980)
XLA Ops:
  0.6 2.7 %shard_map.59 = (f32[9,64,128]{2,1,0:T(8,128)}, f32[9,64,128]{2,1,0:T(8,128)}, f32[6,64,128]{2,1,0:T(8,128)}, f32[6,64,128]{2,1,0:T(8,128)}, f32[3,64,128]{2,1,0:T(8,128)}, /*index=5*/f32[3,64,128]{2,1,0:T(8,128)}) custom-call(f32[12,256,128]{2,1,0:T(8,128)} %bitcast.34, f32[6,256,128]{2,1,0:T(8,128)} %bitcast.28), custom_call_target="tpu_custom_call" | custom-call | flops 3538944 | bytes 3538944 | tf_op jit(solution)/shard_map/pallas_call | solution.py:89
  3.4 5.0 %collective-permute-start.2 = (f32[9,64,128]{2,1,0:T(8,128)}, f32[9,64,128]{2,1,0:T(8,128)S(1)}, u32[]{:S(2)}, u32[]{:S(2)}) collective-permute-start(f32[9,64,128]{2,1,0:T(8,128)} %get-tuple-element.48.refs_3_.refs_1_), channel_id=1, source_target_pairs={{0,4},{4,8},{8,12},{12,16},{16,20},{20,24},{24,28},{1,5},{5,9},{9,... | collective-permute-start | bytes 884744 | tf_op jit(solution)/shard_map/ppermute | solution.py:515
  8.4 1.3 collective-permute-start.3
  9.7 5.7 %shard_map.60 = (f32[256,128]{1,0:T(8,128)}, f32[256,128]{1,0:T(8,128)}) custom-call(f32[12,256,128]{2,1,0:T(8,128)} %bitcast.35, f32[6,256,128]{2,1,0:T(8,128)} %bitcast.29), custom_call_target="tpu_custom_call" | custom-call | flops 2621440 | bytes 2621440 | tf_op jit(solution)/shard_map/pallas_call | solution.py:89
  15.4 1.5 collective-permute-start.4
  16.9 4.4 %collective-permute-start = (f32[6,64,128]{2,1,0:T(8,128)S(1)}, f32[6,64,128]{2,1,0:T(8,128)S(1)}, u32[]{:S(2)}, u32[]{:S(2)}) collective-permute-start(f32[6,64,128]{2,1,0:T(8,128)S(1)} %copy-done.13), channel_id=1, source_target_pairs={{0,4},{4,8},{8,12},{12,16},{16,20},{20,24},{24,28},{1,5},{5,9},{9,... | collective-permute-start | bytes 589832 | tf_op jit(solution)/shard_map/ppermute | solution.py:515
  21.3 1.3 collective-permute-start.1
  22.6 1.3 collective-permute-start.5
  23.9 6.1 %shard_map.62 = (f32[2,24,64,128]{3,2,1,0:T(8,128)}, f32[2,24,64,128]{3,2,1,0:T(8,128)}, f32[8,128]{1,0:T(8,128)}) custom-call(f32[24,256,128]{2,1,0:T(8,128)} %bitcast.23, f32[24,256,128]{2,1,0:T(8,128)} %bitcast.17), custom_call_target="tpu_custom_call" | custom-call | flops 9441280 | bytes 9441280 | tf_op jit(solution)/shard_map/pallas_call | solution.py:89
  30.6 7.7 %shard_map.66 = (f32[6,256,128]{2,1,0:T(8,128)}, f32[2,6,64,128]{3,2,1,0:T(8,128)}, f32[16,8,128]{2,1,0:T(8,128)}) custom-call(f32[12,256,128]{2,1,0:T(8,128)} %bitcast.36, f32[6,256,128]{2,1,0:T(8,128)} %bitcast.30, f32[256,128]{1,0:T(8,128)} %copy-done, f32[256,128]{1,0:T(8,128)} %copy-done.1, f32[256,128]{1,0:T(8,128)} %copy-done, f32[256,128]{1,0:T(8,128)} %copy-done.1, ...), custom_call_target="tpu_custom_call" | custom-call | flops 7274496 | bytes 7274496 | tf_op jit(solution)/shard_map/pallas_call | solution.py:89
  39.1 3.9 %shard_map.67 = (f32[2,6,64,128]{3,2,1,0:T(8,128)}, f32[32,128]{1,0:T(8,128)}) custom-call(f32[9,64,128]{2,1,0:T(8,128)} %get-tuple-element.47.refs_2_.refs_0_, f32[9,64,128]{2,1,0:T(8,128)} %get-tuple-element.48.refs_3_.refs_1_, f32[9,64,128]{2,1,0:T(8,128)} %get-tuple-element.47.refs_2_.refs_0_, f32[9,64,128]{2,1,0:T(8,128)} %get-tuple-element.48.refs_3_.refs_1_, ...), custom_call_target="tpu_custom_call" | custom-call | flops 4800512 | bytes 4800512 | tf_op jit(solution)/shard_map/pallas_call | solution.py:89
  43.1 10.3 %all-to-all-start.1 = ((f32[32,1,128]{2,1,0:T(1,128)}), f32[32,1,128]{2,1,0:T(1,128)S(1)}, u32[]{:S(2)}, u32[]{:S(2)}) async-start(f32[32,1,128]{2,1,0:T(1,128)} %bitcast.44), calls=%async_computation.1 | async-start | bytes 32768 | tf_op jit(solution)/shard_map/all_to_all | solution.py:523
  53.4 7.8 %shard_map.61 = (f32[6,256,128]{2,1,0:T(8,128)}, f32[2,6,64,128]{3,2,1,0:T(8,128)}, f32[16,8,128]{2,1,0:T(8,128)}) custom-call(f32[12,256,128]{2,1,0:T(8,128)} %bitcast.37, f32[6,256,128]{2,1,0:T(8,128)} %bitcast.31, f32[256,128]{1,0:T(8,128)} %copy-done, f32[256,128]{1,0:T(8,128)} %copy-done.1, f32[256,128]{1,0:T(8,128)} %copy-done, f32[256,128]{1,0:T(8,128)} %copy-done.1, ...), custom_call_target="tpu_custom_call" | custom-call | flops 7274496 | bytes 7274496 | tf_op jit(solution)/shard_map/pallas_call | solution.py:89
  61.9 3.9 %shard_map.63 = (f32[2,6,64,128]{3,2,1,0:T(8,128)}, f32[32,128]{1,0:T(8,128)}) custom-call(f32[6,64,128]{2,1,0:T(8,128)} %get-tuple-element.45.refs_0_, f32[6,64,128]{2,1,0:T(8,128)} %get-tuple-element.46.refs_1_, f32[9,64,128]{2,1,0:T(8,128)} %get-tuple-element.47.refs_2_.refs_0_, f32[9,64,128]{2,1,0:T(8,128)} %get-tuple-element.48.refs_3_.refs_1_, ...), custom_call_target="tpu_custom_call" | custom-call | flops 4407296 | bytes 4407296 | tf_op jit(solution)/shard_map/pallas_call | solution.py:89
  65.8 5.8 %all-to-all-start = ((f32[32,1,128]{2,1,0:T(1,128)}), f32[32,1,128]{2,1,0:T(1,128)S(1)}, u32[]{:S(2)}, u32[]{:S(2)}) async-start(f32[32,1,128]{2,1,0:T(1,128)} %bitcast.43), calls=%async_computation | async-start | bytes 32768 | tf_op jit(solution)/shard_map/all_to_all | solution.py:523
  71.6 2.8 %shard_map.68 = (f32[6,64,128]{2,1,0:T(8,128)}, f32[6,64,128]{2,1,0:T(8,128)}) custom-call(f32[32,128]{1,0:T(8,128)} %bitcast.38, f32[2,6,64,128]{3,2,1,0:T(8,128)} %get-tuple-element.69.planes, f32[2,24,64,128]{3,2,1,0:T(8,128)} %get-tuple-element.56.dual_planes.refs_11_), custom_call_target="tpu_custom_call" | custom-call | flops 2375680 | bytes 2375680 | tf_op jit(solution)/shard_map/pallas_call | solution.py:89
  74.5 6.7 %shard_map.69 = (f32[6,256,128]{2,1,0:T(8,128)}, f32[256,128]{1,0:T(8,128)}, f32[256,128]{1,0:T(8,128)}) custom-call(f32[32,128]{1,0:T(8,128)} %bitcast.39, f32[6,256,128]{2,1,0:T(8,128)} %get-tuple-element.68.advanced, f32[24,256,128]{2,1,0:T(8,128)} %bitcast.18, f32[6,64,128]{2,1,0:T(8,128)} %get-tuple-element.70.low_ref.refs_0_, ...), custom_call_target="tpu_custom_call" | custom-call | flops 5390336 | bytes 5390336 | tf_op jit(solution)/shard_map/pallas_call | solution.py:89
  81.2 2.1 %collective-permute-start.12 = (f32[256,128]{1,0:T(8,128)}, f32[256,128]{1,0:T(8,128)S(1)}, u32[]{:S(2)}, u32[]{:S(2)}) collective-permute-start(f32[256,128]{1,0:T(8,128)} %get-tuple-element.73), channel_id=1, source_target_pairs={{0,1},{1,2},{2,3},{4,5},{5,6},{6,7},{8,9},{9,10},{10,11},{12,13},{... | collective-permute-start | bytes 393224 | tf_op jit(solution)/shard_map/ppermute | solution.py:515
  83.4 1.3 collective-permute-start.13
  85.3 2.8 %shard_map.64 = (f32[6,64,128]{2,1,0:T(8,128)}, f32[6,64,128]{2,1,0:T(8,128)}) custom-call(f32[32,128]{1,0:T(8,128)} %bitcast.40, f32[2,6,64,128]{3,2,1,0:T(8,128)} %get-tuple-element.55.planes, f32[2,24,64,128]{3,2,1,0:T(8,128)} %get-tuple-element.56.dual_planes.refs_11_), custom_call_target="tpu_custom_call" | custom-call | flops 2375680 | bytes 2375680 | tf_op jit(solution)/shard_map/pallas_call | solution.py:89
  88.1 6.8 %shard_map.65 = (f32[6,256,128]{2,1,0:T(8,128)}, f32[256,128]{1,0:T(8,128)}, f32[256,128]{1,0:T(8,128)}) custom-call(f32[32,128]{1,0:T(8,128)} %bitcast.41, f32[6,256,128]{2,1,0:T(8,128)} %get-tuple-element.61.advanced, f32[24,256,128]{2,1,0:T(8,128)} %bitcast.19, f32[6,64,128]{2,1,0:T(8,128)} %get-tuple-element.57.low_ref.refs_0_, ...), custom_call_target="tpu_custom_call" | custom-call | flops 5390336 | bytes 5390336 | tf_op jit(solution)/shard_map/pallas_call | solution.py:89
  94.9 4.2 %collective-permute-start.10 = (f32[256,128]{1,0:T(8,128)}, f32[256,128]{1,0:T(8,128)S(1)}, u32[]{:S(2)}, u32[]{:S(2)}) collective-permute-start(f32[256,128]{1,0:T(8,128)} %get-tuple-element.63), channel_id=1, source_target_pairs={{0,1},{1,2},{2,3},{4,5},{5,6},{6,7},{8,9},{9,10},{10,11},{12,13},{... | collective-permute-start | bytes 393224 | tf_op jit(solution)/shard_map/ppermute | solution.py:515
  99.1 3.4 %collective-permute-start.8 = (f32[3,64,128]{2,1,0:T(8,128)S(1)}, f32[3,64,128]{2,1,0:T(8,128)S(1)}, u32[]{:S(2)}, u32[]{:S(2)}) collective-permute-start(f32[3,64,128]{2,1,0:T(8,128)S(1)} %copy-done.9), channel_id=1, source_target_pairs={{0,4},{4,8},{8,12},{12,16},{16,20},{20,24},{24,28},{1,5},{5,9},{9,... | collective-permute-start | bytes 294920 | tf_op jit(solution)/shard_map/ppermute | solution.py:515
  104.9 4.4 %collective-permute-start.14 = (f32[6,64,128]{2,1,0:T(8,128)S(1)}, f32[6,64,128]{2,1,0:T(8,128)S(1)}, u32[]{:S(2)}, u32[]{:S(2)}) collective-permute-start(f32[6,64,128]{2,1,0:T(8,128)S(1)} %copy-done.5), channel_id=1, source_target_pairs={{0,4},{4,8},{8,12},{12,16},{16,20},{20,24},{24,28},{1,5},{5,9},{9,... | collective-permute-start | bytes 589832 | tf_op jit(solution)/shard_map/ppermute | solution.py:515
  109.3 1.3 collective-permute-start.15
  110.6 4.9 %collective-permute-start.6 = (f32[6,64,128]{2,1,0:T(8,128)S(1)}, f32[6,64,128]{2,1,0:T(8,128)S(1)}, u32[]{:S(2)}, u32[]{:S(2)}) collective-permute-start(f32[6,64,128]{2,1,0:T(8,128)S(1)} %copy-done.7), channel_id=1, source_target_pairs={{0,4},{4,8},{8,12},{12,16},{16,20},{20,24},{24,28},{1,5},{5,9},{9,... | collective-permute-start | bytes 589832 | tf_op jit(solution)/shard_map/ppermute | solution.py:515
  118.2 9.4 %shard_map.70 = (f32[6,256,128]{2,1,0:T(8,128)}, f32[2,6,64,128]{3,2,1,0:T(8,128)}, f32[35,8,128]{2,1,0:T(8,128)}) custom-call(f32[6,256,128]{2,1,0:T(8,128)} %get-tuple-element.72.refs_0_, f32[6,256,128]{2,1,0:T(8,128)} %bitcast.32, f32[256,128]{1,0:T(8,128)} %copy-done.22, f32[256,128]{1,0:T(8,128)} %copy-done.23, f32[256,128]{1,0:T(8,128)} %copy-done, ...), custom_call_target="tpu_custom_call" | custom-call | flops 9711616 | bytes 9711616 | tf_op jit(solution)/shard_map/pallas_call | solution.py:89
  127.6 9.6 %shard_map.71 = (f32[6,256,128]{2,1,0:T(8,128)}, f32[2,6,64,128]{3,2,1,0:T(8,128)}, f32[39,8,128]{2,1,0:T(8,128)}) custom-call(f32[6,256,128]{2,1,0:T(8,128)} %get-tuple-element.62.refs_0_, f32[6,256,128]{2,1,0:T(8,128)} %bitcast.33, f32[256,128]{1,0:T(8,128)} %copy-done.24, f32[256,128]{1,0:T(8,128)} %copy-done.25, f32[256,128]{1,0:T(8,128)} %copy-done, ...), custom_call_target="tpu_custom_call" | custom-call | flops 10514432 | bytes 10514432 | tf_op jit(solution)/shard_map/pallas_call | solution.py:89
  138.0 4.8 %shard_map.72 = (f32[2,6,64,128]{3,2,1,0:T(8,128)}, f32[8,128]{1,0:T(8,128)}) custom-call(f32[6,64,128]{2,1,0:T(8,128)} %get-tuple-element.70.low_ref.refs_0_, f32[6,64,128]{2,1,0:T(8,128)} %get-tuple-element.71.high_ref.refs_1_, f32[3,64,128]{2,1,0:T(8,128)} %get-tuple-element.59.refs_2_, f32[3,64,128]{2,1,0:T(8,128)} %get-tuple-element.60.refs_3_, ...), custom_call_target="tpu_custom_call" | custom-call | flops 5259264 | bytes 5259264 | tf_op jit(solution)/shard_map/pallas_call | solution.py:89
  143.6 5.0 %shard_map.73 = (f32[2,6,64,128]{3,2,1,0:T(8,128)}, f32[32,128]{1,0:T(8,128)}) custom-call(f32[6,64,128]{2,1,0:T(8,128)} %get-tuple-element.57.low_ref.refs_0_, f32[6,64,128]{2,1,0:T(8,128)} %get-tuple-element.58.high_ref.refs_1_, f32[3,64,128]{2,1,0:T(8,128)} %get-tuple-element.59.refs_2_, f32[3,64,128]{2,1,0:T(8,128)} %get-tuple-element.60.refs_3_, ...), custom_call_target="tpu_custom_call" | custom-call | flops 5689344 | bytes 5689344 | tf_op jit(solution)/shard_map/pallas_call | solution.py:89
  148.6 17.4 %all_to_all.33 = f32[32,1,128]{2,1,0:T(1,128)} all-to-all(f32[32,1,128]{2,1,0:T(1,128)} %bitcast.45), channel_id=1, replica_groups=mesh['gx'=8,'gy'=4] {'gx','gy'}, dimensions={0} | all-to-all | bytes 32768 | tf_op jit(solution)/shard_map/all_to_all | solution.py:523
  165.9 6.2 %shard_map.74 = (f32[12,256,128]{2,1,0:T(8,128)}, f32[4,4]{1,0:T(4,128)}) custom-call(f32[32,128]{1,0:T(8,128)} %bitcast.42, f32[24,256,128]{2,1,0:T(8,128)} %bitcast.22, f32[6,256,128]{2,1,0:T(8,128)} %get-tuple-element.75.refs_8_.refs_2_, f32[6,256,128]{2,1,0:T(8,128)} %get-tuple-element.84.refs_3_, f32[2,6,64,128]{3,2,1,0:T(8,128)} %get-tuple-element.80.refs_12_.refs_4_, ...), custom_call_target="tpu_custom_call" | custom-call | flops 7094336 | bytes 7094336 | tf_op jit(solution)/shard_map/pallas_call | solution.py:89
  (73 shorter events, 9.3 us)
Async XLA Ops:
  3.4 13.5 %copy-start.13 = (f32[6,64,128]{2,1,0:T(8,128)S(1)}, f32[6,64,128]{2,1,0:T(8,128)}, u32[]{:S(2)}) copy-start(f32[6,64,128]{2,1,0:T(8,128)} %get-tuple-element.46.refs_1_) | copy-start | bytes 589828
  3.4 17.9 %copy-start.12 = (f32[6,64,128]{2,1,0:T(8,128)S(1)}, f32[6,64,128]{2,1,0:T(8,128)}, u32[]{:S(2)}) copy-start(f32[6,64,128]{2,1,0:T(8,128)} %get-tuple-element.45.refs_0_) | copy-start | bytes 589828
  3.4 35.0 %collective-permute-start.2 = (f32[9,64,128]{2,1,0:T(8,128)}, f32[9,64,128]{2,1,0:T(8,128)S(1)}, u32[]{:S(2)}, u32[]{:S(2)}) collective-permute-start(f32[9,64,128]{2,1,0:T(8,128)} %get-tuple-element.48.refs_3_.refs_1_), channel_id=1, source_target_pairs={{0,4},{4,8},{8,12},{12,16},{16,20},{20,24},{24,28},{1,5},{5,9},{9,... | collective-permute-start | bytes 884744 | tf_op jit(solution)/shard_map/ppermute | solution.py:515
  8.4 29.9 %collective-permute-start.3 = (f32[9,64,128]{2,1,0:T(8,128)}, f32[9,64,128]{2,1,0:T(8,128)S(1)}, u32[]{:S(2)}, u32[]{:S(2)}) collective-permute-start(f32[9,64,128]{2,1,0:T(8,128)} %get-tuple-element.47.refs_2_.refs_0_), channel_id=1, source_target_pairs={{4,0},{8,4},{12,8},{16,12},{20,16},{24,20},{28,24},{5,1},{9,5},{13... | collective-permute-start | bytes 884744 | tf_op jit(solution)/shard_map/ppermute | solution.py:515
  15.4 7.2 %collective-permute-start.4 = (f32[256,128]{1,0:T(8,128)}, f32[256,128]{1,0:T(8,128)S(1)}, u32[]{:S(2)}, u32[]{:S(2)}) collective-permute-start(f32[256,128]{1,0:T(8,128)} %get-tuple-element.49), channel_id=1, source_target_pairs={{0,1},{1,2},{2,3},{4,5},{5,6},{6,7},{8,9},{9,10},{10,11},{12,13},{... | collective-permute-start | bytes 393224 | tf_op jit(solution)/shard_map/ppermute | solution.py:515
  16.9 44.3 %collective-permute-start = (f32[6,64,128]{2,1,0:T(8,128)S(1)}, f32[6,64,128]{2,1,0:T(8,128)S(1)}, u32[]{:S(2)}, u32[]{:S(2)}) collective-permute-start(f32[6,64,128]{2,1,0:T(8,128)S(1)} %copy-done.13), channel_id=1, source_target_pairs={{0,4},{4,8},{8,12},{12,16},{16,20},{20,24},{24,28},{1,5},{5,9},{9,... | collective-permute-start | bytes 589832 | tf_op jit(solution)/shard_map/ppermute | solution.py:515
  21.3 39.9 %collective-permute-start.1 = (f32[6,64,128]{2,1,0:T(8,128)S(1)}, f32[6,64,128]{2,1,0:T(8,128)S(1)}, u32[]{:S(2)}, u32[]{:S(2)}) collective-permute-start(f32[6,64,128]{2,1,0:T(8,128)S(1)} %copy-done.12), channel_id=1, source_target_pairs={{4,0},{8,4},{12,8},{16,12},{20,16},{24,20},{28,24},{5,1},{9,5},{13... | collective-permute-start | bytes 589832 | tf_op jit(solution)/shard_map/ppermute | solution.py:515
  22.6 7.4 %copy-start = (f32[256,128]{1,0:T(8,128)}, f32[256,128]{1,0:T(8,128)S(1)}, u32[]{:S(2)}) copy-start(f32[256,128]{1,0:T(8,128)S(1)} %collective-permute-done.4.refs_2_.refs_4_) | copy-start | bytes 393220
  22.6 7.4 %collective-permute-start.5 = (f32[256,128]{1,0:T(8,128)}, f32[256,128]{1,0:T(8,128)S(1)}, u32[]{:S(2)}, u32[]{:S(2)}) collective-permute-start(f32[256,128]{1,0:T(8,128)} %get-tuple-element.50), channel_id=1, source_target_pairs={{1,0},{2,1},{3,2},{5,4},{6,5},{7,6},{9,8},{10,9},{11,10},{13,12},{... | collective-permute-start | bytes 393224 | tf_op jit(solution)/shard_map/ppermute | solution.py:515
  43.1 22.7 %all-to-all-start.1 = ((f32[32,1,128]{2,1,0:T(1,128)}), f32[32,1,128]{2,1,0:T(1,128)S(1)}, u32[]{:S(2)}, u32[]{:S(2)}) async-start(f32[32,1,128]{2,1,0:T(1,128)} %bitcast.44), calls=%async_computation.1 | async-start | bytes 32768 | tf_op jit(solution)/shard_map/all_to_all | solution.py:523
  65.8 18.9 %all-to-all-start = ((f32[32,1,128]{2,1,0:T(1,128)}), f32[32,1,128]{2,1,0:T(1,128)S(1)}, u32[]{:S(2)}, u32[]{:S(2)}) async-start(f32[32,1,128]{2,1,0:T(1,128)} %bitcast.43), calls=%async_computation | async-start | bytes 32768 | tf_op jit(solution)/shard_map/all_to_all | solution.py:523
  81.2 28.1 %collective-permute-start.12 = (f32[256,128]{1,0:T(8,128)}, f32[256,128]{1,0:T(8,128)S(1)}, u32[]{:S(2)}, u32[]{:S(2)}) collective-permute-start(f32[256,128]{1,0:T(8,128)} %get-tuple-element.73), channel_id=1, source_target_pairs={{0,1},{1,2},{2,3},{4,5},{5,6},{6,7},{8,9},{9,10},{10,11},{12,13},{... | collective-permute-start | bytes 393224 | tf_op jit(solution)/shard_map/ppermute | solution.py:515
  83.4 27.2 %collective-permute-start.13 = (f32[256,128]{1,0:T(8,128)}, f32[256,128]{1,0:T(8,128)S(1)}, u32[]{:S(2)}, u32[]{:S(2)}) collective-permute-start(f32[256,128]{1,0:T(8,128)} %get-tuple-element.74), channel_id=1, source_target_pairs={{1,0},{2,1},{3,2},{5,4},{6,5},{7,6},{9,8},{10,9},{11,10},{13,12},{... | collective-permute-start | bytes 393224 | tf_op jit(solution)/shard_map/ppermute | solution.py:515
  88.1 11.0 %copy-start.9 = (f32[3,64,128]{2,1,0:T(8,128)S(1)}, f32[3,64,128]{2,1,0:T(8,128)}, u32[]{:S(2)}) copy-start(f32[3,64,128]{2,1,0:T(8,128)} %get-tuple-element.60.refs_3_) | copy-start | bytes 294916
  88.1 16.8 %copy-start.5 = (f32[6,64,128]{2,1,0:T(8,128)S(1)}, f32[6,64,128]{2,1,0:T(8,128)}, u32[]{:S(2)}) copy-start(f32[6,64,128]{2,1,0:T(8,128)} %get-tuple-element.71.high_ref.refs_1_) | copy-start | bytes 589828
  88.1 21.2 %copy-start.4 = (f32[6,64,128]{2,1,0:T(8,128)S(1)}, f32[6,64,128]{2,1,0:T(8,128)}, u32[]{:S(2)}) copy-start(f32[6,64,128]{2,1,0:T(8,128)} %get-tuple-element.70.low_ref.refs_0_) | copy-start | bytes 589828
  88.1 22.5 %copy-start.7 = (f32[6,64,128]{2,1,0:T(8,128)S(1)}, f32[6,64,128]{2,1,0:T(8,128)}, u32[]{:S(2)}) copy-start(f32[6,64,128]{2,1,0:T(8,128)} %get-tuple-element.58.high_ref.refs_1_) | copy-start | bytes 589828
  88.1 27.4 %copy-start.6 = (f32[6,64,128]{2,1,0:T(8,128)S(1)}, f32[6,64,128]{2,1,0:T(8,128)}, u32[]{:S(2)}) copy-start(f32[6,64,128]{2,1,0:T(8,128)} %get-tuple-element.57.low_ref.refs_0_) | copy-start | bytes 589828
  88.1 28.8 %copy-start.8 = (f32[3,64,128]{2,1,0:T(8,128)S(1)}, f32[3,64,128]{2,1,0:T(8,128)}, u32[]{:S(2)}) copy-start(f32[3,64,128]{2,1,0:T(8,128)} %get-tuple-element.59.refs_2_) | copy-start | bytes 294916
  94.9 20.6 %collective-permute-start.10 = (f32[256,128]{1,0:T(8,128)}, f32[256,128]{1,0:T(8,128)S(1)}, u32[]{:S(2)}, u32[]{:S(2)}) collective-permute-start(f32[256,128]{1,0:T(8,128)} %get-tuple-element.63), channel_id=1, source_target_pairs={{0,1},{1,2},{2,3},{4,5},{5,6},{6,7},{8,9},{9,10},{10,11},{12,13},{... | collective-permute-start | bytes 393224 | tf_op jit(solution)/shard_map/ppermute | solution.py:515
  99.1 5.8 %collective-permute-start.8 = (f32[3,64,128]{2,1,0:T(8,128)S(1)}, f32[3,64,128]{2,1,0:T(8,128)S(1)}, u32[]{:S(2)}, u32[]{:S(2)}) collective-permute-start(f32[3,64,128]{2,1,0:T(8,128)S(1)} %copy-done.9), channel_id=1, source_target_pairs={{0,4},{4,8},{8,12},{12,16},{16,20},{20,24},{24,28},{1,5},{5,9},{9,... | collective-permute-start | bytes 294920 | tf_op jit(solution)/shard_map/ppermute | solution.py:515
  102.5 14.4 %collective-permute-start.11 = (f32[256,128]{1,0:T(8,128)}, f32[256,128]{1,0:T(8,128)S(1)}, u32[]{:S(2)}, u32[]{:S(2)}) collective-permute-start(f32[256,128]{1,0:T(8,128)} %get-tuple-element.64), channel_id=1, source_target_pairs={{1,0},{2,1},{3,2},{5,4},{6,5},{7,6},{9,8},{10,9},{11,10},{13,12},{... | collective-permute-start | bytes 393224 | tf_op jit(solution)/shard_map/ppermute | solution.py:515
  104.9 22.7 %copy-start.10 = (f32[3,64,128]{2,1,0:T(8,128)}, f32[3,64,128]{2,1,0:T(8,128)S(1)}, u32[]{:S(2)}) copy-start(f32[3,64,128]{2,1,0:T(8,128)S(1)} %collective-permute-done.8.refs_6_) | copy-start | bytes 294916
  104.9 32.4 %collective-permute-start.14 = (f32[6,64,128]{2,1,0:T(8,128)S(1)}, f32[6,64,128]{2,1,0:T(8,128)S(1)}, u32[]{:S(2)}, u32[]{:S(2)}) collective-permute-start(f32[6,64,128]{2,1,0:T(8,128)S(1)} %copy-done.5), channel_id=1, source_target_pairs={{0,4},{4,8},{8,12},{12,16},{16,20},{20,24},{24,28},{1,5},{5,9},{9,... | collective-permute-start | bytes 589832 | tf_op jit(solution)/shard_map/ppermute | solution.py:515
  109.3 8.9 %copy-start.22 = (f32[256,128]{1,0:T(8,128)}, f32[256,128]{1,0:T(8,128)S(1)}, u32[]{:S(2)}) copy-start(f32[256,128]{1,0:T(8,128)S(1)} %collective-permute-done.12.refs_2_) | copy-start | bytes 393220
  109.3 28.0 %collective-permute-start.15 = (f32[6,64,128]{2,1,0:T(8,128)S(1)}, f32[6,64,128]{2,1,0:T(8,128)S(1)}, u32[]{:S(2)}, u32[]{:S(2)}) collective-permute-start(f32[6,64,128]{2,1,0:T(8,128)S(1)} %copy-done.4), channel_id=1, source_target_pairs={{4,0},{8,4},{12,8},{16,12},{20,16},{24,20},{28,24},{5,1},{9,5},{13... | collective-permute-start | bytes 589832 | tf_op jit(solution)/shard_map/ppermute | solution.py:515
  110.6 7.6 %copy-start.23 = (f32[256,128]{1,0:T(8,128)}, f32[256,128]{1,0:T(8,128)S(1)}, u32[]{:S(2)}) copy-start(f32[256,128]{1,0:T(8,128)S(1)} %collective-permute-done.13.refs_3_) | copy-start | bytes 393220
  110.6 32.2 %collective-permute-start.6 = (f32[6,64,128]{2,1,0:T(8,128)S(1)}, f32[6,64,128]{2,1,0:T(8,128)S(1)}, u32[]{:S(2)}, u32[]{:S(2)}) collective-permute-start(f32[6,64,128]{2,1,0:T(8,128)S(1)} %copy-done.7), channel_id=1, source_target_pairs={{0,4},{4,8},{8,12},{12,16},{16,20},{20,24},{24,28},{1,5},{5,9},{9,... | collective-permute-start | bytes 589832 | tf_op jit(solution)/shard_map/ppermute | solution.py:515
  115.5 12.0 %copy-start.24 = (f32[256,128]{1,0:T(8,128)}, f32[256,128]{1,0:T(8,128)S(1)}, u32[]{:S(2)}) copy-start(f32[256,128]{1,0:T(8,128)S(1)} %collective-permute-done.10.refs_2_) | copy-start | bytes 393220
  115.6 27.3 %collective-permute-start.7 = (f32[6,64,128]{2,1,0:T(8,128)S(1)}, f32[6,64,128]{2,1,0:T(8,128)S(1)}, u32[]{:S(2)}, u32[]{:S(2)}) collective-permute-start(f32[6,64,128]{2,1,0:T(8,128)S(1)} %copy-done.6), channel_id=1, source_target_pairs={{4,0},{8,4},{12,8},{16,12},{20,16},{24,20},{28,24},{5,1},{9,5},{13... | collective-permute-start | bytes 589832 | tf_op jit(solution)/shard_map/ppermute | solution.py:515
  116.9 10.7 %copy-start.25 = (f32[256,128]{1,0:T(8,128)}, f32[256,128]{1,0:T(8,128)S(1)}, u32[]{:S(2)}) copy-start(f32[256,128]{1,0:T(8,128)S(1)} %collective-permute-done.11.refs_3_) | copy-start | bytes 393220
  116.9 20.3 %collective-permute-start.9 = (f32[3,64,128]{2,1,0:T(8,128)S(1)}, f32[3,64,128]{2,1,0:T(8,128)S(1)}, u32[]{:S(2)}, u32[]{:S(2)}) collective-permute-start(f32[3,64,128]{2,1,0:T(8,128)S(1)} %copy-done.8), channel_id=1, source_target_pairs={{4,0},{8,4},{12,8},{16,12},{20,16},{24,20},{28,24},{5,1},{9,5},{13... | collective-permute-start | bytes 294920 | tf_op jit(solution)/shard_map/ppermute | solution.py:515
  (12 other events, 13.6 us)
where the time goes:
time: 173 us; the launch traced here: 172 us
  Pallas kernels  92 us (53%)
  starting transfers between devices  56.3 us (33%)
  blocking collectives  17.4 us (10%)
  local copies, waits for them, and re-layouts  4.32 us (2%)
    pallas_call x16, Pallas kernels, call(): pl.pallas_call(kernel, out_shape=[jax.ShapeDtypeStruct(shape, jnp.float32...  92 us
    ppermute x16, starting transfers between devices, shift(): lax.ppermute(field, axis, pairs if up else [(j, i) for i, j in pairs])  40.2 us
    all_to_all x1, blocking collectives, exchange(): return lax.all_to_all(payload, ('gx', 'gy'), 0, 0, tiled=True)  17.4 us
    all_to_all x2, starting transfers between devices, exchange(): return lax.all_to_all(payload, ('gx', 'gy'), 0, 0, tiled=True)  16.1 us
    unnamed x52, local copies, waits for them, and re-layouts  4.32 us
  transfers between devices with their start and end apart: 18, of which 1 were waited for; matrix products, arithmetic and copies ran while one was open for 0% of the time, Pallas kernels for 45%

commit v1 on v0

v1 whole, which is shorter than its diff:
```python
import functools
import math

import jax
import jax.numpy as jnp
from jax import lax
from jax.experimental import pallas as pl
from jax.experimental.pallas import tpu as pltpu
from jax.sharding import PartitionSpec as P

step_size = 0.1
viscosity = 0.2
HALF = 0.5 * step_size
DIFF = step_size * viscosity
SUB = 8
LANES = 128


def lane_ids():
    return lax.broadcasted_iota(jnp.int32, (SUB, LANES), 1)


def row_ids():
    return lax.broadcasted_iota(jnp.int32, (SUB, LANES), 0)


def roll(x, shift, axis):
    shift %= x.shape[axis]
    return x if shift == 0 else pltpu.roll(x, shift, axis)


def block(ref, field, k):
    return ref[field, pl.ds(pl.multiple_of(k * SUB, SUB), SUB), :]


def put_block(ref, field, k, value):
    ref[field, pl.ds(pl.multiple_of(k * SUB, SUB), SUB), :] = value


def pairs_of(n):
    return [(i, j) for i in range(n) for j in range(i, n)]


def lane_sums(slots):
    half, lane = LANES // 2, lane_ids()
    while len(slots) > 1:
        count = len(slots) // 2
        low = (lane & half) == 0
        merged = []
        for one, two in zip(slots[:count], slots[count:]):
            if one is None and two is None:
                merged.append(None)
            elif two is None:
                merged.append(one + roll(one, -half, 1))
            elif one is None:
                merged.append(two + roll(two, half, 1))
            else:
                kept = jnp.where(low, one, two)
                moved = jnp.where(low, roll(one, -half, 1), roll(two, half, 1))
                merged.append(kept + moved)
        slots, half = merged, half // 2
    total = slots[0]
    while half >= 1:
        total = total + roll(total, half, 1)
        half //= 2
    for shift in (4, 2, 1):
        total = total + roll(total, shift, 0)
    return total


def spread(total, lane):
    return jnp.broadcast_to(total[:, lane : lane + 1], (SUB, LANES))


def gathered_total(ref):
    total = ref[0:SUB, :]
    for first in range(SUB, ref.shape[0], SUB):
        total = total + ref[first : first + SUB, :]
    for shift in (4, 2, 1):
        total = total + roll(total, shift, 0)
    return total


def call(kernel, micros, outs, *args, scratch=(), any_args=()):
    specs = [
        pl.BlockSpec(memory_space=pl.ANY if i in any_args else pltpu.VMEM) for i in range(len(args))
    ]
    shapes = [a.shape for i, a in enumerate(args) if i not in any_args] + list(outs)
    shapes += [ref.shape for ref in scratch if ref is not pltpu.SemaphoreType.DMA]
    held = sum(4 * math.prod((*shape[:-1], LANES)) for shape in shapes)
    return pl.pallas_call(
        kernel,
        out_shape=[jax.ShapeDtypeStruct(shape, jnp.float32) for shape in outs],
        in_specs=specs,
        out_specs=[pl.BlockSpec(memory_space=pltpu.VMEM) for _ in outs],
        scratch_shapes=list(scratch),
        compiler_params=pltpu.CompilerParams(vmem_limit_bytes=held + (2 << 20)),
        cost_estimate=pl.CostEstimate(
            flops=0, bytes_accessed=int(micros * 3.5e6), transcendentals=0
        ),
    )(*args)


def sides(width):
    even = lax.rem(lax.axis_index("gx"), 2) == 0
    first = jnp.where(even, width - 1, 0)
    sign = jnp.where(even, 1.0, -1.0)
    return (first, width - 1 - first), (sign, -sign)


def pack_y(fields, first_ref, second_ref, blocks):
    lane = lane_ids()
    even = lax.rem(lax.axis_index("gy"), 2) == 0

    def step(k, carry):
        left = jnp.zeros((SUB, LANES), jnp.float32)
        right = left
        for n, (ref, f) in enumerate(fields):
            value = block(ref, f, k)
            left = jnp.where(lane == (2 * n - 1) % LANES, roll(value, 2 * n - 1, 1), left)
            right = jnp.where(lane == 2 * n, roll(value, 2 * n + 1, 1), right)
        rows = pl.ds(pl.multiple_of(k * SUB, SUB), SUB)
        first_ref[rows, :] = jnp.where(even, right, left)
        second_ref[rows, :] = jnp.where(even, left, right)
        return carry

    lax.fori_loop(0, blocks, step, 0, unroll=4)


def pack_x_kernel(width, sets, q_ref, base_ref, *outs):
    layers, _ = sides(width)
    for fields, pair in zip(sets, zip(outs[::2], outs[1::2])):
        for out, x in zip(pair, layers):
            for n, (which, f) in enumerate(fields):
                ref = (q_ref, base_ref)[which]
                out[n] = ref[f, pl.ds(x, out.shape[1], stride=width), :]


def pack_y_kernel(q_ref, base_ref, first_ref, second_ref):
    fields = [(q_ref, f) for f in range(q_ref.shape[0])]
    fields += [(base_ref, f) for f in range(base_ref.shape[0])]
    pack_y(fields, first_ref, second_ref, q_ref.shape[1] // SUB)


def modes_kernel(width, modes, slot, direct_ref, dual_ref, direct_planes, dual_planes, metric_ref):
    depth = direct_planes.shape[2]
    comps = direct_ref.shape[0] // modes
    layers, _ = sides(width)
    for ref, planes in ((direct_ref, direct_planes), (dual_ref, dual_planes)):
        for f in range(ref.shape[0]):
            for side, x in enumerate(layers):
                planes[side, f] = ref[f, pl.ds(x, depth, stride=width), :]
    todo = pairs_of(modes)
    slots = [None] * LANES

    def step(k, accs):
        accs = list(accs)
        for c in range(comps):
            values = [block(dual_ref, m * comps + c, k) for m in range(modes)]
            for n, (a, b) in enumerate(todo):
                accs[n] = accs[n] + values[a] * values[b]
        return tuple(accs)

    zero = jnp.zeros((SUB, LANES), jnp.float32)
    sums = lax.fori_loop(0, dual_ref.shape[1] // SUB, step, (zero,) * len(todo))
    for n, value in enumerate(sums):
        slots[slot + n] = value
    lane = lane_ids()
    inside = (lane >= slot) & (lane < slot + len(todo))
    metric_ref[...] = jnp.where(inside, lane_sums(slots), 0.0)


def advance_kernel(width, comps, base_at, base_y, projections, *refs):
    q_ref, base_ref, hq_l, hq_r, hb_l, hb_r = refs[:6]
    mode_refs = refs[6 : 6 + projections]
    out_ref, planes_ref, sums_ref = refs[6 + projections :]
    fields, rows = out_ref.shape[:2]
    vectors, blocks = fields // comps, rows // SUB
    depth = rows // width
    lane, row = lane_ids(), row_ids()
    x_at = row % width
    low_x = jnp.where(x_at > 0, 1.0, 0.0)
    high_x = jnp.where(x_at < width - 1, 1.0, 0.0)
    upper = row < width

    def around(ref, f, k, before, after, halo, lane_at):
        here = block(ref, f, k)
        edge = roll(halo, -lane_at, 1)
        y_low = jnp.where(lane == 0, edge, roll(here, 1, 1))
        y_high = jnp.where(lane == LANES - 1, edge, roll(here, -1, 1))
        x_low, x_high = roll(here, 1, 0), roll(here, -1, 0)
        z_low, z_high = z_neighbours(here, block(ref, f, before), block(ref, f, after))
        return here, (x_low, y_low, z_low), (x_high, y_high, z_high)

    def z_neighbours(here, earlier, later):
        shift = SUB - width
        if shift == 0:
            return earlier, later
        low = roll(jnp.where(row < SUB - width, here, earlier), width, 0)
        high = roll(jnp.where(row < width, later, here), -width, 0)
        return low, high

    def step(k, carry):
        before = lax.rem(k + blocks - 1, blocks)
        after = lax.rem(k + 1, blocks)
        rows_k = pl.ds(pl.multiple_of(k * SUB, SUB), SUB)
        halo_q = hq_l[rows_k, :] + hq_r[rows_k, :]
        halo_b = hb_l[rows_k, :] + hb_r[rows_k, :]
        centre, grads = [], []
        for j in range(comps):
            here, low, high = around(base_ref, base_at + j, k, before, after, halo_b, 2 * (base_y + j))
            centre.append(HALF * here)
            grads.append(
                (
                    HALF * (high[0] * high_x - low[0] * low_x),
                    HALF * (high[1] - low[1]),
                    HALF * (high[2] - low[2]),
                )
            )
        plus = [(DIFF + centre[0]) * high_x, DIFF + centre[1], DIFF + centre[2]]
        minus = [(DIFF - centre[0]) * low_x, DIFF - centre[1], DIFF - centre[2]]
        for v in range(vectors):
            values = []
            sums = []
            for c in range(comps):
                f = v * comps + c
                here, low, high = around(
                    q_ref, f, k, before, after, halo_q, 2 * f
                )
                total = (1.0 - 6.0 * DIFF) * here
                for d in range(3):
                    total = total + plus[d] * high[d] + minus[d] * low[d]
                values.append(here)
                sums.append(total)
            for c in range(comps):
                total = sums[c]
                for j in range(comps):
                    total = total - values[j] * grads[j][c]
                put_block(out_ref, v * comps + c, k, total)
        return carry

    lax.fori_loop(0, blocks, step, 0)
    layers, _ = sides(width)
    for f in range(fields):
        for side, x in enumerate(layers):
            planes_ref[side, f] = out_ref[f, pl.ds(x, depth, stride=width), :]

    zero = jnp.zeros((SUB, LANES), jnp.float32)
    at = 0
    for ref in mode_refs:
        modes = ref.shape[0] // comps

        def dots(k, accs):
            accs = list(accs)
            for c in range(comps):
                right = [block(out_ref, v * comps + c, k) for v in range(vectors)]
                for m in range(modes):
                    left = block(ref, m * comps + c, k)
                    for v in range(vectors):
                        accs[m * vectors + v] = accs[m * vectors + v] + left * right[v]
            return tuple(accs)

        for value in lax.fori_loop(0, blocks, dots, (zero,) * (modes * vectors)):
            sums_ref[at] = value
            at += 1
    if sums_ref.shape[0] > at:
        keep = (x_at > 0) & (x_at < width - 1)
        own = pairs_of(vectors)

        def gram(k, accs):
            accs = list(accs)
            for c in range(comps):
                inner = [jnp.where(keep, block(out_ref, v * comps + c, k), 0.0) for v in range(vectors)]
                for n, (i, j) in enumerate(own):
                    accs[n] = accs[n] + inner[i] * inner[j]
            return tuple(accs)

        for value in lax.fori_loop(0, blocks, gram, (zero,) * len(own)):
            sums_ref[at] = value
            at += 1


def edge_kernel(width, comps, at, lanes, projections, extra, *refs):
    own_q, own_b, halo_q, halo_b = (refs[n : n + 2] for n in (0, 2, 4, 6))
    advanced, sums_ref = refs[8:10]
    mode_refs, refs = refs[10 : 10 + projections], refs[10 + projections :]
    extra_refs, (new_ref, payload_ref) = refs[:extra], refs[extra:]
    fields, depth = new_ref.shape[1:3]
    vectors, blocks = fields // comps, depth // SUB
    _, signs = sides(width)

    def step(k, carry):
        rows = pl.ds(pl.multiple_of(k * SUB, SUB), SUB)
        for side in range(2):
            scale = signs[side] * HALF
            factor = DIFF + scale * own_b[side][at[0], rows, :]
            outer = [scale * halo_b[side][at[1] + j, rows, :] for j in range(comps)]
            for v in range(vectors):
                for c in range(comps):
                    value = factor * halo_q[side][v * comps + c, rows, :]
                    if c == 0:
                        for j in range(comps):
                            value = value - own_q[side][v * comps + j, rows, :] * outer[j]
                    new_ref[side, v * comps + c, rows, :] = value
        return carry

    lax.fori_loop(0, blocks, step, 0)
    at_sum = 0
    slots = {}
    for n, ref in enumerate(mode_refs):
        modes = ref.shape[1] // comps
        accs = tuple(sums_ref[at_sum + i] for i in range(modes * vectors))
        at_sum += modes * vectors

        def dots(k, accs, ref=ref):
            accs = list(accs)
            rows = pl.ds(pl.multiple_of(k * SUB, SUB), SUB)
            for side in range(2):
                for c in range(comps):
                    right = [new_ref[side, v * comps + c, rows, :] for v in range(vectors)]
                    for m in range(modes):
                        left = ref[side, m * comps + c, rows, :]
                        for v in range(vectors):
                            accs[m * vectors + v] = accs[m * vectors + v] + left * right[v]
            return tuple(accs)

        for lane, value in zip(lanes[n], lax.fori_loop(0, blocks, dots, accs)):
            slots[lane] = value
    own = pairs_of(vectors)
    squares = at_sum < sums_ref.shape[0]
    accs = tuple(sums_ref[at_sum + i] for i in range(len(own))) if squares else ()

    def finish(k, accs):
        accs = list(accs)
        rows = pl.ds(pl.multiple_of(k * SUB, SUB), SUB)
        for side in range(2):
            for c in range(comps):
                inner = []
                for v in range(vectors):
                    f = v * comps + c
                    inner.append(new_ref[side, f, rows, :] + advanced[side, f, rows, :])
                    new_ref[side, f, rows, :] = inner[v]
                if squares:
                    for n, (i, j) in enumerate(own):
                        accs[n] = accs[n] + inner[i] * inner[j]
        return tuple(accs)

    for lane, value in zip(lanes[-1] if squares else (), lax.fori_loop(0, blocks, finish, accs)):
        slots[lane] = value
    lane = lane_ids()
    inside = lane < 0
    for position in slots:
        inside = inside | (lane == position)
    total = jnp.where(inside, lane_sums([slots.get(i) for i in range(LANES)]), 0.0)
    for ref in extra_refs:
        total = total + ref[...]
    for first in range(0, payload_ref.shape[0], SUB):
        payload_ref[first : first + SUB, :] = total


def deflate_planes_kernel(comps, lanes, gathered, planes, dual_planes, first_ref, second_ref, factors):
    total = gathered_total(gathered)
    for i, lane in enumerate(lanes):
        factors[i] = spread(total, lane)
    fields, depth = first_ref.shape[:2]
    vectors = fields // comps
    modes = dual_planes.shape[1] // comps
    for side, out in ((0, first_ref), (1, second_ref)):

        def step(k, carry, side=side, out=out):
            rows = pl.ds(pl.multiple_of(k * SUB, SUB), SUB)
            for c in range(comps):
                values = [planes[side, v * comps + c, rows, :] for v in range(vectors)]
                for m in range(modes):
                    mode = dual_planes[side, m * comps + c, rows, :]
                    for v in range(vectors):
                        values[v] = values[v] - factors[m * vectors + v] * mode
                for v in range(vectors):
                    out[v * comps + c, rows, :] = values[v]
            return carry

        lax.fori_loop(0, depth // SUB, step, 0)


def deflate_kernel(
    width, comps, lanes, gathered, advanced, dual, planes_a, planes_b, out_ref, first_ref, second_ref, factors
):
    total = gathered_total(gathered)
    for i, lane in enumerate(lanes):
        factors[i] = spread(total, lane)
    fields, rows_all = out_ref.shape[:2]
    vectors = fields // comps
    modes = dual.shape[0] // comps

    def step(k, carry):
        for c in range(comps):
            values = [block(advanced, v * comps + c, k) for v in range(vectors)]
            for m in range(modes):
                mode = block(dual, m * comps + c, k)
                for v in range(vectors):
                    values[v] = values[v] - factors[m * vectors + v] * mode
            for v in range(vectors):
                put_block(out_ref, v * comps + c, k, values[v])
        return carry

    lax.fori_loop(0, rows_all // SUB, step, 0)
    depth = rows_all // width
    layers, _ = sides(width)
    for f in range(fields):
        for planes, x in zip((planes_a, planes_b), layers):
            out_ref[f, pl.ds(x, depth, stride=width), :] = planes[f]
    pack_y([(out_ref, f) for f in range(fields)], first_ref, second_ref, rows_all // SUB)


def finish_kernel(width, comps, layout, scale, *refs):
    gathered, dual, advanced, planes, out_ref, growth_ref, block_ref, factors, semaphore = refs
    fields, rows_all = out_ref.shape[:2]
    vectors, modes = fields // comps, dual.shape[0] // comps
    copy = pltpu.make_async_copy(advanced, block_ref, semaphore)
    copy.start()
    total = gathered_total(gathered)
    first, cross, self_gram, metric = layout
    coef = {key: spread(total, lane) for key, lane in first.items()}
    mixed = {key: spread(total, lane) for key, lane in cross.items()}
    inner = {key: spread(total, lane) for key, lane in self_gram.items()}
    weight = {key: spread(total, lane) for key, lane in metric.items()}
    weighted = {}
    for m in range(modes):
        for j in range(vectors):
            weighted[m, j] = sum(weight[min(m, n), max(m, n)] * coef[n, j] for n in range(modes))
    gram = {}
    for i, j in pairs_of(vectors):
        value = inner[i, j]
        for m in range(modes):
            value = value - coef[m, i] * (mixed[m, j] - weighted[m, j]) - coef[m, j] * mixed[m, i]
        gram[j, i] = value
    lower, inverse_diagonal = {}, {}
    for j in range(vectors):
        value = gram[j, j]
        for n in range(j):
            value = value - lower[j, n] * lower[j, n]
        lower[j, j] = jnp.sqrt(value)
        inverse_diagonal[j] = 1.0 / lower[j, j]
        for i in range(j + 1, vectors):
            value = gram[i, j]
            for n in range(j):
                value = value - lower[i, n] * lower[j, n]
            lower[i, j] = value * inverse_diagonal[j]
    inverse = {}
    for j in range(vectors):
        inverse[j, j] = inverse_diagonal[j]
        for i in range(j + 1, vectors):
            value = sum(lower[i, n] * inverse[n, j] for n in range(j, i))
            inverse[i, j] = -inverse_diagonal[i] * value
    row, lane = row_ids(), lane_ids()
    growth = jnp.zeros((SUB, LANES), jnp.float32)
    for (i, j), value in lower.items():
        growth = jnp.where((row == i) & (lane == j), value, growth)
    growth_ref[...] = growth[:vectors, :vectors]
    at = {}
    for (i, j), value in inverse.items():
        at[i, j] = len(at)
        factors[at[i, j]] = scale * value
    mode_at = {}
    for i in range(vectors):
        for m in range(modes):
            mode_at[i, m] = len(at) + len(mode_at)
            factors[mode_at[i, m]] = -scale * sum(inverse[i, j] * coef[m, j] for j in range(i + 1))
    copy.wait()
    depth = rows_all // width
    layers, _ = sides(width)
    for f in range(fields):
        for side, x in enumerate(layers):
            block_ref[f, pl.ds(x, depth, stride=width), :] = planes[side, f]

    def step(k, carry):
        for c in range(comps):
            parts = [block(block_ref, v * comps + c, k) for v in range(vectors)]
            values = []
            for i in range(vectors):
                value = factors[at[i, 0]] * parts[0]
                for j in range(1, i + 1):
                    value = value + factors[at[i, j]] * parts[j]
                values.append(value)
            for m in range(modes):
                mode = block(dual, m * comps + c, k)
                for i in range(vectors):
                    values[i] = values[i] + factors[mode_at[i, m]] * mode
            for i in range(vectors):
                put_block(out_ref, i * comps + c, k, values[i])
        return carry

    lax.fori_loop(0, rows_all // SUB, step, 0)


def swap(first, second, axis):
    count = lax.axis_size(axis)
    results = []
    for field, start in ((first, 0), (second, 1)):
        pairs = [(i, i + 1) for i in range(start, count - 1, 2)]
        results.append(lax.ppermute(field, axis, pairs + [(j, i) for i, j in pairs]))
    return results


def exchange(payload):
    return lax.all_to_all(payload, ("gx", "gy"), 0, 0, tiled=True)


def body(adjoint_block, base_flow, direct_modes, dual_modes):
    vectors, comps, depth, width, length = adjoint_block.shape
    steps, modes = base_flow.shape[0], direct_modes.shape[0]
    rows = depth * width
    assert length == LANES and SUB % width == 0 and rows % SUB == 0 and depth % SUB == 0
    devices = lax.axis_size("gx") * lax.axis_size("gy")
    cells = float(comps * rows * length * devices)
    fields = vectors * comps

    q = adjoint_block.reshape(fields, rows, length)
    base = base_flow.reshape(steps * comps, rows, length)
    direct = direct_modes.reshape(modes * comps, rows, length)
    dual = dual_modes.reshape(modes * comps, rows, length)
    plane = (depth, length)

    sets = [
        [(0, f) for f in range(fields)] + [(1, j) for j in range(comps)],
        [(1, comps + j) for j in range(comps)],
    ]
    *layers, late_a, late_b = call(
        functools.partial(pack_x_kernel, width, sets),
        2.5,
        [(len(some), *plane) for some in sets for _ in range(2)],
        q,
        base,
    )
    halo_x = swap(*layers, "gx")
    halo_y = swap(*call(pack_y_kernel, 3, [(rows, LANES)] * 2, q, base), "gy")

    pairs, mode_pairs = pairs_of(vectors), pairs_of(modes)
    first = {(m, i): m * vectors + i for m in range(modes) for i in range(vectors)}
    cross = {key: modes * vectors + lane for key, lane in first.items()}
    self_gram = {key: 2 * modes * vectors + n for n, key in enumerate(pairs)}
    slot = 2 * modes * vectors + len(pairs)
    metric = {key: slot + n for n, key in enumerate(mode_pairs)}
    assert slot + len(mode_pairs) <= LANES
    direct_planes, dual_planes, metric_part = call(
        functools.partial(modes_kernel, width, modes, slot),
        4,
        [(2, modes * comps, *plane)] * 2 + [(SUB, LANES)],
        direct,
        dual,
    )

    spacing = LANES // (1 << (modes * vectors - 1).bit_length())
    spaced = [spacing * n for n in range(modes * vectors)]
    advanced, planes, sums = call(
        functools.partial(advance_kernel, width, comps, 0, fields, 1),
        8,
        [(fields, rows, length), (2, fields, *plane), (modes * vectors, SUB, LANES)],
        q,
        base,
        *halo_y,
        *halo_y,
        direct,
    )
    edge, payload = call(
        functools.partial(edge_kernel, width, comps, (fields, fields), [spaced], 1, 0),
        2,
        [(2, fields, *plane), (devices, LANES)],
        *layers,
        *layers,
        *halo_x,
        *halo_x,
        planes,
        sums,
        direct_planes,
    )
    payload, late_a, late_b = lax.optimization_barrier((payload, late_a, late_b))
    halo_late = swap(late_a, late_b, "gx")
    gathered = exchange(payload)

    scratch = [pltpu.VMEM((modes * vectors, SUB, LANES), jnp.float32)]
    layers = call(
        functools.partial(deflate_planes_kernel, comps, spaced),
        1.5,
        [(fields, *plane)] * 2,
        gathered,
        edge,
        dual_planes,
        scratch=scratch,
    )
    halo_x = swap(*layers, "gx")
    current, *columns = call(
        functools.partial(deflate_kernel, width, comps, spaced),
        3,
        [(fields, rows, length), (rows, LANES), (rows, LANES)],
        gathered,
        advanced,
        dual,
        *layers,
        scratch=scratch,
    )
    columns = swap(*columns, "gy")
    advanced, planes, sums = call(
        functools.partial(advance_kernel, width, comps, comps, fields + comps, 2),
        12,
        [(fields, rows, length), (2, fields, *plane), (2 * modes * vectors + len(pairs), SUB, LANES)],
        current,
        base,
        *columns,
        *halo_y,
        direct,
        dual,
    )
    lanes = [list(first.values()), list(cross.values()), list(self_gram.values())]
    edge, payload = call(
        functools.partial(edge_kernel, width, comps, (0, 0), lanes, 2, 1),
        3,
        [(2, fields, *plane), (devices, LANES)],
        *layers,
        late_a,
        late_b,
        *halo_x,
        *halo_late,
        planes,
        sums,
        direct_planes,
        dual_planes,
        metric_part,
    )
    total = exchange(payload)
    factor_count = vectors * (vectors + 1) // 2 + modes * vectors
    next_block, growth = call(
        functools.partial(finish_kernel, width, comps, (first, cross, self_gram, metric), math.sqrt(cells)),
        5,
        [(fields, rows, length), (vectors, vectors)],
        total,
        dual,
        advanced,
        edge,
        scratch=[
            pltpu.VMEM((fields, rows, length), jnp.float32),
            pltpu.VMEM((factor_count, SUB, LANES), jnp.float32),
            pltpu.SemaphoreType.DMA,
        ],
        any_args=(2,),
    )
    return (next_block.reshape(adjoint_block.shape), growth)


def solution(mesh):
    placed = P(None, None, None, "gx", "gy")
    return jax.shard_map(
        body,
        mesh=mesh,
        in_specs=(placed,) * 4,
        out_specs=(placed, P()),
        check_vma=False,
    )
```

time: 173 us -> 80 us (0.46)
  Pallas kernels: 92 us -> 26.6 us
  starting transfers between devices: 56.3 us -> 10.5 us
  waiting for transfers between devices: 1.15 us -> 11.9 us
  blocking collectives: 17.4 us -> 22.8 us
  local copies, waits for them, and re-layouts: 4.32 us -> 6.97 us
    pallas_call x16 -> x10, Pallas kernels: 92 us -> 26.6 us  [call(): pl.pallas_call(kernel, out_shape=[jax.ShapeDtypeStruct(shape, jnp.float32...]
    ppermute x16 -> x10, starting transfers between devices: 40.2 us -> 10.5 us  [swap(): lax.ppermute(field, axis, pairs + [(j, i) for i, j in pairs])]
    all_to_all x2 -> x0, starting transfers between devices: 16.1 us -> none  [exchange(): return lax.all_to_all(payload, ('gx', 'gy'), 0, 0, tiled=True)]
    ppermute x16 -> x10, waiting for transfers between devices: 1.14 us -> 11.9 us  [swap(): lax.ppermute(field, axis, pairs + [(j, i) for i, j in pairs])]
    all_to_all x1 -> x2, blocking collectives: 17.4 us -> 22.8 us  [exchange(): return lax.all_to_all(payload, ('gx', 'gy'), 0, 0, tiled=True)]
    unnamed x52 -> x18, local copies, waits for them, and re-layouts: 4.32 us -> 6.97 us
  transfers between devices with their start and end apart: 18 -> 10, of which waited for: 1 -> 2; matrix products, arithmetic and copies ran while one was open for 0% -> 0% of each run, Pallas kernels for 45% -> 24%
where the time goes in v1:
time: 80 us; the launch traced here: 79.6 us
  Pallas kernels  26.6 us (33%)
  blocking collectives  22.8 us (28%)
  waiting for transfers between devices  11.9 us (15%)
  starting transfers between devices  10.5 us (13%)
  local copies, waits for them, and re-layouts  6.97 us (9%)
  between operations  0.83 us (1%)
    pallas_call x10, Pallas kernels, call(): pl.pallas_call(kernel, out_shape=[jax.ShapeDtypeStruct(shape, jnp.float32...  26.6 us
    all_to_all x2, blocking collectives, exchange(): return lax.all_to_all(payload, ('gx', 'gy'), 0, 0, tiled=True)  22.8 us
    ppermute x10, waiting for transfers between devices, swap(): lax.ppermute(field, axis, pairs + [(j, i) for i, j in pairs])  11.9 us
    ppermute x10, starting transfers between devices, swap(): lax.ppermute(field, axis, pairs + [(j, i) for i, j in pairs])  10.5 us
    unnamed x18, local copies, waits for them, and re-layouts  6.97 us
  transfers between devices with their start and end apart: 10, of which 2 were waited for; matrix products, arithmetic and copies ran while one was open for 0% of the time, Pallas kernels for 24%

profile of v1, /device:TPU:0, one launch (start us, length us, event | category | flops | bytes accessed | tf_op | source)
XLA Modules:
  0.0 79.6 jit_solution(40733597165904380)
XLA Ops:
  0.6 0.0 copy-start.3
  0.6 1.4 %copy-done.3 = f32[4,3,64,4,128]{4,3,2,1,0:T(4,128)S(1)} copy-done((f32[4,3,64,4,128]{4,3,2,1,0:T(4,128)S(1)}, f32[4,3,64,4,128]{4,3,2,1,0:T(4,128)}, u32[]{:S(2)}) %copy-start.3) | copy-done | bytes 1572888
  2.0 1.1 %copy-done.6 = f32[2,3,64,4,128]{4,3,2,1,0:T(4,128)S(1)} copy-done((f32[2,3,64,4,128]{4,3,2,1,0:T(4,128)S(1)}, f32[2,3,64,4,128]{4,3,2,1,0:T(4,128)}, u32[]{:S(2)}) %copy-start.6) | copy-done | bytes 786456
  3.2 0.2 shard_map.59
  3.3 3.0 %collective-permute-start = (f32[15,64,128]{2,1,0:T(8,128)S(1)}, f32[15,64,128]{2,1,0:T(8,128)S(1)}, u32[]{:S(2)}, u32[]{:S(2)}) collective-permute-start(f32[15,64,128]{2,1,0:T(8,128)S(1)} %get-tuple-element.31.refs_0_.refs_2_), channel_id=1, source_target_pairs={{0,4},{8,12},{16,20},{24,28},{4,0},{12,8},{20,16},{28,24},{1,5},{9... | collective-permute-start | bytes 1474568 | tf_op jit(solution)/shard_map/ppermute | solution.py:501
  6.4 0.7 collective-permute-start.1
  7.1 0.0 copy-start.4
  7.1 1.4 %copy-done.4 = f32[4,3,64,4,128]{4,3,2,1,0:T(4,128)S(1)} copy-done((f32[4,3,64,4,128]{4,3,2,1,0:T(4,128)S(1)}, f32[4,3,64,4,128]{4,3,2,1,0:T(4,128)}, u32[]{:S(2)}) %copy-start.4) | copy-done | bytes 1572888
  8.5 1.1 %copy-done.7 = f32[2,3,64,4,128]{4,3,2,1,0:T(4,128)S(1)} copy-done((f32[2,3,64,4,128]{4,3,2,1,0:T(4,128)S(1)}, f32[2,3,64,4,128]{4,3,2,1,0:T(4,128)}, u32[]{:S(2)}) %copy-start.7) | copy-done | bytes 786456
  9.6 1.8 %shard_map.60 = (f32[256,128]{1,0:T(8,128)S(1)}, f32[256,128]{1,0:T(8,128)S(1)}) custom-call(f32[12,256,128]{2,1,0:T(8,128)S(1)} %bitcast.21, f32[6,256,128]{2,1,0:T(8,128)S(1)} %bitcast.24), custom_call_target="tpu_custom_call" | custom-call | bytes 10500000 | tf_op jit(solution)/shard_map/pallas_call | solution.py:91
  11.4 0.1 collective-permute-start.2
  11.4 0.7 collective-permute-start.3
  12.1 1.9 %copy-done.1 = f32[8,3,64,4,128]{4,3,2,1,0:T(4,128)S(1)} copy-done((f32[8,3,64,4,128]{4,3,2,1,0:T(4,128)S(1)}, f32[8,3,64,4,128]{4,3,2,1,0:T(4,128)}, u32[]{:S(2)}) %copy-start.1) | copy-done | bytes 3145752
  14.0 2.2 %shard_map.62 = (f32[2,24,64,128]{3,2,1,0:T(8,128)S(1)}, f32[2,24,64,128]{3,2,1,0:T(8,128)S(1)}, f32[8,128]{1,0:T(8,128)S(1)}) custom-call(f32[24,256,128]{2,1,0:T(8,128)S(1)} %bitcast.17, f32[24,256,128]{2,1,0:T(8,128)S(1)} %bitcast.13), custom_call_target="tpu_custom_call" | custom-call | bytes 14000000 | tf_op jit(solution)/shard_map/pallas_call | solution.py:91
  16.2 0.0 collective-permute-done.2.refs_2_.refs_4_
  16.3 5.1 %shard_map.61 = (f32[12,256,128]{2,1,0:T(8,128)S(1)}, f32[2,12,64,128]{3,2,1,0:T(8,128)S(1)}, f32[32,8,128]{2,1,0:T(8,128)S(1)}) custom-call(f32[12,256,128]{2,1,0:T(8,128)S(1)} %bitcast.22, f32[6,256,128]{2,1,0:T(8,128)S(1)} %bitcast.25, f32[256,128]{1,0:T(8,128)S(1)} %collective-permute-done.2.refs_2_.refs_4_, ...), custom_call_target="tpu_custom_call" | custom-call | bytes 28000000 | tf_op jit(solution)/shard_map/pallas_call | solution.py:91
  21.4 6.0 %collective-permute-done.refs_4_.refs_6_ = f32[15,64,128]{2,1,0:T(8,128)S(1)} collective-permute-done((f32[15,64,128]{2,1,0:T(8,128)S(1)}, f32[15,64,128]{2,1,0:T(8,128)S(1)}, u32[]{:S(2)}, u32[]{:S(2)}) %collective-permute-start) | collective-permute-done | bytes 491552 | tf_op jit(solution)/shard_map/ppermute | solution.py:501
  27.4 1.5 %shard_map.63 = (f32[2,12,64,128]{3,2,1,0:T(8,128)S(1)}, f32[32,128]{1,0:T(8,128)S(1)}) custom-call(f32[15,64,128]{2,1,0:T(8,128)S(1)} %get-tuple-element.31.refs_0_.refs_2_, f32[15,64,128]{2,1,0:T(8,128)S(1)} %get-tuple-element.32.refs_1_.refs_3_, f32[15,64,128]{2,1,0:T(8,128)S(1)} %get-tuple-element.31.refs_0_.refs_2_, ...), custom_call_target="tpu_custom_call" | custom-call | bytes 7000000 | tf_op jit(solution)/shard_map/pallas_call | solution.py:91
  28.9 12.9 %all_to_all.22 = f32[32,1,128]{2,1,0:T(1,128)S(1)} all-to-all(f32[32,1,128]{2,1,0:T(1,128)S(1)} %bitcast.31), channel_id=1, replica_groups=mesh['gx'=8,'gy'=4] {'gx','gy'}, dimensions={0} | all-to-all | bytes 32768 | tf_op jit(solution)/shard_map/all_to_all | solution.py:506
  41.8 0.8 shard_map.64
  42.6 0.6 collective-permute-start.4
  43.2 0.7 collective-permute-start.5
  43.9 2.9 %shard_map.65 = (f32[12,256,128]{2,1,0:T(8,128)S(1)}, f32[256,128]{1,0:T(8,128)S(1)}, f32[256,128]{1,0:T(8,128)S(1)}) custom-call(f32[32,128]{1,0:T(8,128)S(1)} %bitcast.28, f32[12,256,128]{2,1,0:T(8,128)S(1)} %get-tuple-element.48.advanced, f32[24,256,128]{2,1,0:T(8,128)S(1)} %bitcast.14, f32[12,64,128]{2,1,0:T(8,128)S(1)} %get-tuple-element.44.planes_a.refs_0_, ...), custom_call_target="tpu_custom_call" | custom-call | bytes 10500000 | tf_op jit(solution)/shard_map/pallas_call | solution.py:91
  46.8 0.1 collective-permute-start.8
  46.9 0.7 collective-permute-start.9
  47.6 3.3 %collective-permute-start.6 = (f32[3,64,128]{2,1,0:T(8,128)S(1)}, f32[3,64,128]{2,1,0:T(8,128)S(1)}, u32[]{:S(2)}, u32[]{:S(2)}) collective-permute-start(f32[3,64,128]{2,1,0:T(8,128)S(1)} %get-tuple-element.46.refs_2_), channel_id=1, source_target_pairs={{0,4},{8,12},{16,20},{24,28},{4,0},{12,8},{20,16},{28,24},{1,5},{9... | collective-permute-start | bytes 294920 | tf_op jit(solution)/shard_map/ppermute | solution.py:501
  50.9 0.7 collective-permute-start.7
  51.6 6.8 %shard_map.66 = (f32[12,256,128]{2,1,0:T(8,128)S(1)}, f32[2,12,64,128]{3,2,1,0:T(8,128)S(1)}, f32[74,8,128]{2,1,0:T(8,128)S(1)}) custom-call(f32[12,256,128]{2,1,0:T(8,128)S(1)} %get-tuple-element.49.refs_0_, f32[6,256,128]{2,1,0:T(8,128)S(1)} %bitcast.26, f32[256,128]{1,0:T(8,128)S(1)} %collective-permute-done.8.refs_2_, ...), custom_call_target="tpu_custom_call" | custom-call | bytes 42000000 | tf_op jit(solution)/shard_map/pallas_call | solution.py:91
  58.3 5.9 %collective-permute-done.6.refs_6_ = f32[3,64,128]{2,1,0:T(8,128)S(1)} collective-permute-done((f32[3,64,128]{2,1,0:T(8,128)S(1)}, f32[3,64,128]{2,1,0:T(8,128)S(1)}, u32[]{:S(2)}, u32[]{:S(2)}) %collective-permute-start.6) | collective-permute-done | bytes 98336 | tf_op jit(solution)/shard_map/ppermute | solution.py:501
  64.2 2.2 %shard_map.67 = (f32[2,12,64,128]{3,2,1,0:T(8,128)S(1)}, f32[32,128]{1,0:T(8,128)S(1)}) custom-call(f32[12,64,128]{2,1,0:T(8,128)S(1)} %get-tuple-element.44.planes_a.refs_0_, f32[12,64,128]{2,1,0:T(8,128)S(1)} %get-tuple-element.45.planes_b.refs_1_, f32[3,64,128]{2,1,0:T(8,128)S(1)} %get-tuple-element.46.refs_2_, ...), custom_call_target="tpu_custom_call" | custom-call | bytes 10500000 | tf_op jit(solution)/shard_map/pallas_call | solution.py:91
  66.4 9.9 %all_to_all.23 = f32[32,1,128]{2,1,0:T(1,128)S(1)} all-to-all(f32[32,1,128]{2,1,0:T(1,128)S(1)} %bitcast.30), channel_id=1, replica_groups=mesh['gx'=8,'gy'=4] {'gx','gy'}, dimensions={0} | all-to-all | bytes 32768 | tf_op jit(solution)/shard_map/all_to_all | solution.py:506
  76.3 3.3 %shard_map.68 = (f32[12,256,128]{2,1,0:T(8,128)}, f32[4,4]{1,0:T(4,128)}) custom-call(f32[32,128]{1,0:T(8,128)S(1)} %bitcast.29, f32[24,256,128]{2,1,0:T(8,128)S(1)} %bitcast.16, f32[12,256,128]{2,1,0:T(8,128)S(1)} %get-tuple-element.56.refs_2_, f32[2,12,64,128]{3,2,1,0:T(8,128)S(1)} %get-tuple-element.57.refs_3_), custom_call_target="tpu_custom_call" | custom-call | bytes 17500000 | tf_op jit(solution)/shard_map/pallas_call | solution.py:91
  (18 shorter events, 0.0 us)
Async XLA Ops:
  0.6 1.4 %copy-start.3 = (f32[4,3,64,4,128]{4,3,2,1,0:T(4,128)S(1)}, f32[4,3,64,4,128]{4,3,2,1,0:T(4,128)}, u32[]{:S(2)}) copy-start(f32[4,3,64,4,128]{4,3,2,1,0:T(4,128)} %param.4) | copy-start | bytes 4718596
  2.0 1.1 %copy-start.6 = (f32[2,3,64,4,128]{4,3,2,1,0:T(4,128)S(1)}, f32[2,3,64,4,128]{4,3,2,1,0:T(4,128)}, u32[]{:S(2)}) copy-start(f32[2,3,64,4,128]{4,3,2,1,0:T(4,128)} %param.5) | copy-start | bytes 2359300
  3.2 9.0 %copy-start = (f32[8,3,64,4,128]{4,3,2,1,0:T(4,128)S(1)}, f32[8,3,64,4,128]{4,3,2,1,0:T(4,128)}, u32[]{:S(2)}) copy-start(f32[8,3,64,4,128]{4,3,2,1,0:T(4,128)} %param.7) | copy-start | bytes 9437188
  3.3 24.0 %collective-permute-start = (f32[15,64,128]{2,1,0:T(8,128)S(1)}, f32[15,64,128]{2,1,0:T(8,128)S(1)}, u32[]{:S(2)}, u32[]{:S(2)}) collective-permute-start(f32[15,64,128]{2,1,0:T(8,128)S(1)} %get-tuple-element.31.refs_0_.refs_2_), channel_id=1, source_target_pairs={{0,4},{8,12},{16,20},{24,28},{4,0},{12,8},{20,16},{28,24},{1,5},{9... | collective-permute-start | bytes 1474568 | tf_op jit(solution)/shard_map/ppermute | solution.py:501
  6.4 21.0 %collective-permute-start.1 = (f32[15,64,128]{2,1,0:T(8,128)S(1)}, f32[15,64,128]{2,1,0:T(8,128)S(1)}, u32[]{:S(2)}, u32[]{:S(2)}) collective-permute-start(f32[15,64,128]{2,1,0:T(8,128)S(1)} %get-tuple-element.32.refs_1_.refs_3_), channel_id=1, source_target_pairs={{4,8},{12,16},{20,24},{8,4},{16,12},{24,20},{5,9},{13,17},{21,25},... | collective-permute-start | bytes 1474568 | tf_op jit(solution)/shard_map/ppermute | solution.py:501
  7.1 1.4 %copy-start.4 = (f32[4,3,64,4,128]{4,3,2,1,0:T(4,128)S(1)}, f32[4,3,64,4,128]{4,3,2,1,0:T(4,128)}, u32[]{:S(2)}) copy-start(f32[4,3,64,4,128]{4,3,2,1,0:T(4,128)} %param.4) | copy-start | bytes 4718596
  8.5 1.1 %copy-start.7 = (f32[2,3,64,4,128]{4,3,2,1,0:T(4,128)S(1)}, f32[2,3,64,4,128]{4,3,2,1,0:T(4,128)}, u32[]{:S(2)}) copy-start(f32[2,3,64,4,128]{4,3,2,1,0:T(4,128)} %param.5) | copy-start | bytes 2359300
  11.4 4.9 %collective-permute-start.2 = (f32[256,128]{1,0:T(8,128)S(1)}, f32[256,128]{1,0:T(8,128)S(1)}, u32[]{:S(2)}, u32[]{:S(2)}) collective-permute-start(f32[256,128]{1,0:T(8,128)S(1)} %get-tuple-element.33), channel_id=1, source_target_pairs={{0,1},{2,3},{1,0},{3,2},{4,5},{6,7},{5,4},{7,6},{8,9},{10,11},{9,8... | collective-permute-start | bytes 393224 | tf_op jit(solution)/shard_map/ppermute | solution.py:501
  11.4 4.8 %collective-permute-start.3 = (f32[256,128]{1,0:T(8,128)S(1)}, f32[256,128]{1,0:T(8,128)S(1)}, u32[]{:S(2)}, u32[]{:S(2)}) collective-permute-start(f32[256,128]{1,0:T(8,128)S(1)} %get-tuple-element.34), channel_id=1, source_target_pairs={{1,2},{2,1},{5,6},{6,5},{9,10},{10,9},{13,14},{14,13},{17,18},{18,... | collective-permute-start | bytes 393224 | tf_op jit(solution)/shard_map/ppermute | solution.py:501
  12.1 1.9 %copy-start.1 = (f32[8,3,64,4,128]{4,3,2,1,0:T(4,128)S(1)}, f32[8,3,64,4,128]{4,3,2,1,0:T(4,128)}, u32[]{:S(2)}) copy-start(f32[8,3,64,4,128]{4,3,2,1,0:T(4,128)} %param.6) | copy-start | bytes 9437188
  14.0 2.2 %copy-start.5 = (f32[4,3,64,4,128]{4,3,2,1,0:T(4,128)S(1)}, f32[4,3,64,4,128]{4,3,2,1,0:T(4,128)}, u32[]{:S(2)}) copy-start(f32[4,3,64,4,128]{4,3,2,1,0:T(4,128)} %param.4) | copy-start | bytes 4718596
  14.0 2.2 %copy-start.8 = (f32[2,3,64,4,128]{4,3,2,1,0:T(4,128)S(1)}, f32[2,3,64,4,128]{4,3,2,1,0:T(4,128)}, u32[]{:S(2)}) copy-start(f32[2,3,64,4,128]{4,3,2,1,0:T(4,128)} %param.5) | copy-start | bytes 2359300
  42.6 21.6 %collective-permute-start.4 = (f32[12,64,128]{2,1,0:T(8,128)S(1)}, f32[12,64,128]{2,1,0:T(8,128)S(1)}, u32[]{:S(2)}, u32[]{:S(2)}) collective-permute-start(f32[12,64,128]{2,1,0:T(8,128)S(1)} %get-tuple-element.44.planes_a.refs_0_), channel_id=1, source_target_pairs={{0,4},{8,12},{16,20},{24,28},{4,0},{12,8},{20,16},{28,24},{1,5},{9... | collective-permute-start | bytes 1179656 | tf_op jit(solution)/shard_map/ppermute | solution.py:501
  43.2 21.0 %collective-permute-start.5 = (f32[12,64,128]{2,1,0:T(8,128)S(1)}, f32[12,64,128]{2,1,0:T(8,128)S(1)}, u32[]{:S(2)}, u32[]{:S(2)}) collective-permute-start(f32[12,64,128]{2,1,0:T(8,128)S(1)} %get-tuple-element.45.planes_b.refs_1_), channel_id=1, source_target_pairs={{4,8},{12,16},{20,24},{8,4},{16,12},{24,20},{5,9},{13,17},{21,25},... | collective-permute-start | bytes 1179656 | tf_op jit(solution)/shard_map/ppermute | solution.py:501
  43.9 7.7 %copy-start.2 = (f32[8,3,64,4,128]{4,3,2,1,0:T(4,128)S(1)}, f32[8,3,64,4,128]{4,3,2,1,0:T(4,128)}, u32[]{:S(2)}) copy-start(f32[8,3,64,4,128]{4,3,2,1,0:T(4,128)} %param.6) | copy-start | bytes 9437188
  46.8 4.1 %collective-permute-start.8 = (f32[256,128]{1,0:T(8,128)S(1)}, f32[256,128]{1,0:T(8,128)S(1)}, u32[]{:S(2)}, u32[]{:S(2)}) collective-permute-start(f32[256,128]{1,0:T(8,128)S(1)} %get-tuple-element.50), channel_id=1, source_target_pairs={{0,1},{2,3},{1,0},{3,2},{4,5},{6,7},{5,4},{7,6},{8,9},{10,11},{9,8... | collective-permute-start | bytes 393224 | tf_op jit(solution)/shard_map/ppermute | solution.py:501
  46.9 4.7 %collective-permute-start.9 = (f32[256,128]{1,0:T(8,128)S(1)}, f32[256,128]{1,0:T(8,128)S(1)}, u32[]{:S(2)}, u32[]{:S(2)}) collective-permute-start(f32[256,128]{1,0:T(8,128)S(1)} %get-tuple-element.51), channel_id=1, source_target_pairs={{1,2},{2,1},{5,6},{6,5},{9,10},{10,9},{13,14},{14,13},{17,18},{18,... | collective-permute-start | bytes 393224 | tf_op jit(solution)/shard_map/ppermute | solution.py:501
  47.6 16.6 %collective-permute-start.6 = (f32[3,64,128]{2,1,0:T(8,128)S(1)}, f32[3,64,128]{2,1,0:T(8,128)S(1)}, u32[]{:S(2)}, u32[]{:S(2)}) collective-permute-start(f32[3,64,128]{2,1,0:T(8,128)S(1)} %get-tuple-element.46.refs_2_), channel_id=1, source_target_pairs={{0,4},{8,12},{16,20},{24,28},{4,0},{12,8},{20,16},{28,24},{1,5},{9... | collective-permute-start | bytes 294920 | tf_op jit(solution)/shard_map/ppermute | solution.py:501
  50.9 13.3 %collective-permute-start.7 = (f32[3,64,128]{2,1,0:T(8,128)S(1)}, f32[3,64,128]{2,1,0:T(8,128)S(1)}, u32[]{:S(2)}, u32[]{:S(2)}) collective-permute-start(f32[3,64,128]{2,1,0:T(8,128)S(1)} %get-tuple-element.47.refs_3_), channel_id=1, source_target_pairs={{4,8},{12,16},{20,24},{8,4},{16,12},{24,20},{5,9},{13,17},{21,25},... | collective-permute-start | bytes 294920 | tf_op jit(solution)/shard_map/ppermute | solution.py:501

commit v2 on v1

--- a/solution.py
+++ b/solution.py
@@ -7,6 +7,7 @@
 from jax.experimental import pallas as pl
 from jax.experimental.pallas import tpu as pltpu
 from jax.sharding import PartitionSpec as P
+
 
 step_size = 0.1
 viscosity = 0.2
@@ -81,18 +82,24 @@
     return total
 
 
-def call(kernel, micros, outs, *args, scratch=(), any_args=()):
+def call(kernel, micros, outs, *args, scratch=(), hbm_args=(), hbm_outs=()):
     specs = [
-        pl.BlockSpec(memory_space=pl.ANY if i in any_args else pltpu.VMEM) for i in range(len(args))
+        pl.BlockSpec(memory_space=pltpu.HBM if i in hbm_args else pltpu.VMEM) for i in range(len(args))
     ]
-    shapes = [a.shape for i, a in enumerate(args) if i not in any_args] + list(outs)
-    shapes += [ref.shape for ref in scratch if ref is not pltpu.SemaphoreType.DMA]
+    shapes = [a.shape for i, a in enumerate(args) if i not in hbm_args]
+    shapes += [shape for i, shape in enumerate(outs) if i not in hbm_outs]
+    shapes += [ref.shape for ref in scratch if ref.memory_space == pltpu.VMEM]
     held = sum(4 * math.prod((*shape[:-1], LANES)) for shape in shapes)
+    args = [
+        pltpu.with_memory_space_constraint(a, pltpu.HBM) if i in hbm_args else a for i, a in enumerate(args)
+    ]
     return pl.pallas_call(
         kernel,
         out_shape=[jax.ShapeDtypeStruct(shape, jnp.float32) for shape in outs],
         in_specs=specs,
-        out_specs=[pl.BlockSpec(memory_space=pltpu.VMEM) for _ in outs],
+        out_specs=[
+            pl.BlockSpec(memory_space=pltpu.HBM if i in hbm_outs else pltpu.VMEM) for i in range(len(outs))
+        ],
         scratch_shapes=list(scratch),
         compiler_params=pltpu.CompilerParams(vmem_limit_bytes=held + (2 << 20)),
         cost_estimate=pl.CostEstimate(
@@ -127,13 +134,22 @@
     lax.fori_loop(0, blocks, step, 0, unroll=4)
 
 
-def pack_x_kernel(width, sets, q_ref, base_ref, *outs):
+def pack_x_kernel(width, sets, q_hbm, base_hbm, q_ref, base_ref, *outs):
+    outs, semaphore = outs[:-1], outs[-1]
     layers, _ = sides(width)
+    sources, held = (q_hbm, base_hbm), (q_ref, base_ref)
+    order = [field for fields in sets for field in fields]
+    copies = {
+        (which, f): pltpu.make_async_copy(sources[which].at[f], held[which].at[f], semaphore.at[n])
+        for n, (which, f) in enumerate(order)
+    }
+    for copy in copies.values():
+        copy.start()
     for fields, pair in zip(sets, zip(outs[::2], outs[1::2])):
-        for out, x in zip(pair, layers):
-            for n, (which, f) in enumerate(fields):
-                ref = (q_ref, base_ref)[which]
-                out[n] = ref[f, pl.ds(x, out.shape[1], stride=width), :]
+        for n, (which, f) in enumerate(fields):
+            copies[which, f].wait()
+            for out, x in zip(pair, layers):
+                out[n] = held[which][f, pl.ds(x, out.shape[1], stride=width), :]
 
 
 def pack_y_kernel(q_ref, base_ref, first_ref, second_ref):
@@ -181,7 +197,6 @@
     x_at = row % width
     low_x = jnp.where(x_at > 0, 1.0, 0.0)
     high_x = jnp.where(x_at < width - 1, 1.0, 0.0)
-    upper = row < width
 
     def around(ref, f, k, before, after, halo, lane_at):
         here = block(ref, f, k)
@@ -280,106 +295,125 @@
             at += 1
 
 
-def edge_kernel(width, comps, at, lanes, projections, extra, *refs):
-    own_q, own_b, halo_q, halo_b = (refs[n : n + 2] for n in (0, 2, 4, 6))
-    advanced, sums_ref = refs[8:10]
-    mode_refs, refs = refs[10 : 10 + projections], refs[10 + projections :]
-    extra_refs, (new_ref, payload_ref) = refs[:extra], refs[extra:]
-    fields, depth = new_ref.shape[1:3]
+def edge_kernel(width, comps, side, at, lanes, projections, extra, *refs):
+    own_q, own_b, halo_q, halo_b, advanced, sums_ref = refs[:6]
+    mode_refs, refs = refs[6 : 6 + projections], refs[6 + projections :]
+    extra_refs, (new_ref, result_ref) = refs[:extra], refs[extra:]
+    fields, depth = new_ref.shape[:2]
     vectors, blocks = fields // comps, depth // SUB
-    _, signs = sides(width)
+    scale = sides(width)[1][side] * HALF
 
     def step(k, carry):
         rows = pl.ds(pl.multiple_of(k * SUB, SUB), SUB)
-        for side in range(2):
-            scale = signs[side] * HALF
-            factor = DIFF + scale * own_b[side][at[0], rows, :]
-            outer = [scale * halo_b[side][at[1] + j, rows, :] for j in range(comps)]
-            for v in range(vectors):
-                for c in range(comps):
-                    value = factor * halo_q[side][v * comps + c, rows, :]
-                    if c == 0:
-                        for j in range(comps):
-                            value = value - own_q[side][v * comps + j, rows, :] * outer[j]
-                    new_ref[side, v * comps + c, rows, :] = value
+        factor = DIFF + scale * own_b[at[0], rows, :]
+        outer = [scale * halo_b[at[1] + j, rows, :] for j in range(comps)]
+        for v in range(vectors):
+            for c in range(comps):
+                value = factor * halo_q[v * comps + c, rows, :]
+                if c == 0:
+                    for j in range(comps):
+                        value = value - own_q[v * comps + j, rows, :] * outer[j]
+                new_ref[v * comps + c, rows, :] = value
         return carry
 
     lax.fori_loop(0, blocks, step, 0)
-    at_sum = 0
-    slots = {}
-    for n, ref in enumerate(mode_refs):
+    total = []
+    for ref in mode_refs:
         modes = ref.shape[1] // comps
-        accs = tuple(sums_ref[at_sum + i] for i in range(modes * vectors))
-        at_sum += modes * vectors
+        accs = tuple(sums_ref[len(total) + i] for i in range(modes * vectors))
 
         def dots(k, accs, ref=ref):
             accs = list(accs)
             rows = pl.ds(pl.multiple_of(k * SUB, SUB), SUB)
-            for side in range(2):
-                for c in range(comps):
-                    right = [new_ref[side, v * comps + c, rows, :] for v in range(vectors)]
-                    for m in range(modes):
-                        left = ref[side, m * comps + c, rows, :]
-                        for v in range(vectors):
-                            accs[m * vectors + v] = accs[m * vectors + v] + left * right[v]
+            for c in range(comps):
+                right = [new_ref[v * comps + c, rows, :] for v in range(vectors)]
+                for m in range(modes):
+                    left = ref[side, m * comps + c, rows, :]
+                    for v in range(vectors):
+                        accs[m * vectors + v] = accs[m * vectors + v] + left * right[v]
             return tuple(accs)
 
-        for lane, value in zip(lanes[n], lax.fori_loop(0, blocks, dots, accs)):
-            slots[lane] = value
+        total += lax.fori_loop(0, blocks, dots, accs)
     own = pairs_of(vectors)
-    squares = at_sum < sums_ref.shape[0]
-    accs = tuple(sums_ref[at_sum + i] for i in range(len(own))) if squares else ()
+    squares = len(total) < sums_ref.shape[0]
+    accs = tuple(sums_ref[len(total) + i] for i in range(len(own))) if squares else ()
 
     def finish(k, accs):
         accs = list(accs)
         rows = pl.ds(pl.multiple_of(k * SUB, SUB), SUB)
-        for side in range(2):
-            for c in range(comps):
-                inner = []
-                for v in range(vectors):
-                    f = v * comps + c
-                    inner.append(new_ref[side, f, rows, :] + advanced[side, f, rows, :])
-                    new_ref[side, f, rows, :] = inner[v]
-                if squares:
-                    for n, (i, j) in enumerate(own):
-                        accs[n] = accs[n] + inner[i] * inner[j]
+        for c in range(comps):
+            inner = []
+            for v in range(vectors):
+                f = v * comps + c
+                inner.append(new_ref[f, rows, :] + advanced[side, f, rows, :])
+                new_ref[f, rows, :] = inner[v]
+            if squares:
+                for n, (i, j) in enumerate(own):
+                    accs[n] = accs[n] + inner[i] * inner[j]
         return tuple(accs)
 
-    for lane, value in zip(lanes[-1] if squares else (), lax.fori_loop(0, blocks, finish, accs)):
-        slots[lane] = value
+    total += lax.fori_loop(0, blocks, finish, accs)
+    if lanes is None:
+        for n, value in enumerate(total):
+            result_ref[n] = value
+        return
+    slots = dict(zip(lanes, total))
     lane = lane_ids()
     inside = lane < 0
     for position in slots:
         inside = inside | (lane == position)
-    total = jnp.where(inside, lane_sums([slots.get(i) for i in range(LANES)]), 0.0)
+    packed = jnp.where(inside, lane_sums([slots.get(i) for i in range(LANES)]), 0.0)
     for ref in extra_refs:
-        total = total + ref[...]
-    for first in range(0, payload_ref.shape[0], SUB):
-        payload_ref[first : first + SUB, :] = total
-
-
-def deflate_planes_kernel(comps, lanes, gathered, planes, dual_planes, first_ref, second_ref, factors):
+        packed = packed + ref[...]
+    for first in range(0, result_ref.shape[0], SUB):
+        result_ref[first : first + SUB, :] = packed
+
+
+def edges(width, comps, at, lanes, micros, devices, own_q, own_b, halo_q, halo_b, advanced, sums, modes, extra):
+    layers = []
+    for side in range(2):
+        last = side == 1
+        kernel = functools.partial(
+            edge_kernel, width, comps, side, at, lanes if last else None, len(modes), len(extra) if last else 0
+        )
+        new, sums = call(
+            kernel,
+            micros,
+            [advanced.shape[1:], (devices, LANES) if last else sums.shape],
+            own_q[side],
+            own_b[side],
+            halo_q[side],
+            halo_b[side],
+            advanced,
+            sums,
+            *modes,
+            *(extra if last else ()),
+        )
+        layers.append(new)
+    return layers, sums
+
+
+def deflate_planes_kernel(comps, lanes, side, gathered, planes, dual_planes, out, factors):
     total = gathered_total(gathered)
     for i, lane in enumerate(lanes):
         factors[i] = spread(total, lane)
-    fields, depth = first_ref.shape[:2]
+    fields, depth = out.shape[:2]
     vectors = fields // comps
     modes = dual_planes.shape[1] // comps
-    for side, out in ((0, first_ref), (1, second_ref)):
-
-        def step(k, carry, side=side, out=out):
-            rows = pl.ds(pl.multiple_of(k * SUB, SUB), SUB)
-            for c in range(comps):
-                values = [planes[side, v * comps + c, rows, :] for v in range(vectors)]
-                for m in range(modes):
-                    mode = dual_planes[side, m * comps + c, rows, :]
-                    for v in range(vectors):
-                        values[v] = values[v] - factors[m * vectors + v] * mode
+
+    def step(k, carry):
+        rows = pl.ds(pl.multiple_of(k * SUB, SUB), SUB)
+        for c in range(comps):
+            values = [planes[v * comps + c, rows, :] for v in range(vectors)]
+            for m in range(modes):
+                mode = dual_planes[side, m * comps + c, rows, :]
                 for v in range(vectors):
-                    out[v * comps + c, rows, :] = values[v]
-            return carry
-
-        lax.fori_loop(0, depth // SUB, step, 0)
+                    values[v] = values[v] - factors[m * vectors + v] * mode
+            for v in range(vectors):
+                out[v * comps + c, rows, :] = values[v]
+        return carry
+
+    lax.fori_loop(0, depth // SUB, step, 0)
 
 
 def deflate_kernel(
@@ -413,11 +447,11 @@
 
 
 def finish_kernel(width, comps, layout, scale, *refs):
-    gathered, dual, advanced, planes, out_ref, growth_ref, block_ref, factors, semaphore = refs
+    gathered, dual, advanced, *planes, out_hbm, growth_ref, out_ref, factors, semaphore = refs
     fields, rows_all = out_ref.shape[:2]
     vectors, modes = fields // comps, dual.shape[0] // comps
-    copy = pltpu.make_async_copy(advanced, block_ref, semaphore)
-    copy.start()
+    depth = rows_all // width
+    layers, _ = sides(width)
     total = gathered_total(gathered)
     first, cross, self_gram, metric = layout
     coef = {key: spread(total, lane) for key, lane in first.items()}
@@ -466,16 +500,17 @@
         for m in range(modes):
             mode_at[i, m] = len(at) + len(mode_at)
             factors[mode_at[i, m]] = -scale * sum(inverse[i, j] * coef[m, j] for j in range(i + 1))
-    copy.wait()
-    depth = rows_all // width
-    layers, _ = sides(width)
     for f in range(fields):
-        for side, x in enumerate(layers):
-            block_ref[f, pl.ds(x, depth, stride=width), :] = planes[side, f]
+        for own, x in zip(planes, layers):
+            out_ref[f, pl.ds(x, depth, stride=width), :] = own[f]
+    outer = (row % width == 0) | (row % width == width - 1)
 
     def step(k, carry):
         for c in range(comps):
-            parts = [block(block_ref, v * comps + c, k) for v in range(vectors)]
+            parts = []
+            for v in range(vectors):
+                inner = block(advanced, v * comps + c, k)
+                parts.append(jnp.where(outer, block(out_ref, v * comps + c, k), inner))
             values = []
             for i in range(vectors):
                 value = factors[at[i, 0]] * parts[0]
@@ -490,7 +525,17 @@
                 put_block(out_ref, i * comps + c, k, values[i])
         return carry
 
-    lax.fori_loop(0, rows_all // SUB, step, 0)
+    chunks = semaphore.shape[0]
+    size = rows_all // SUB // chunks
+    copies = []
+    for n in range(chunks):
+        lax.fori_loop(n * size, (n + 1) * size, step, 0)
+        rows = pl.ds(n * size * SUB, size * SUB)
+        copy = pltpu.make_async_copy(out_ref.at[:, rows], out_hbm.at[:, rows], semaphore.at[n])
+        copy.start()
+        copies.append(copy)
+    for copy in copies:
+        copy.wait()
 
 
 def swap(first, second, axis):
@@ -525,14 +570,17 @@
         [(0, f) for f in range(fields)] + [(1, j) for j in range(comps)],
         [(1, comps + j) for j in range(comps)],
     ]
-    *layers, late_a, late_b = call(
+    q, base, *layers, late_a, late_b = call(
         functools.partial(pack_x_kernel, width, sets),
-        2.5,
-        [(len(some), *plane) for some in sets for _ in range(2)],
+        1.5,
+        [q.shape, base.shape] + [(len(some), *plane) for some in sets for _ in range(2)],
         q,
         base,
+        scratch=[pltpu.SemaphoreType.DMA((fields + steps * comps,))],
+        hbm_args=(0, 1),
     )
     halo_x = swap(*layers, "gx")
+    halo_late = swap(late_a, late_b, "gx")
     halo_y = swap(*call(pack_y_kernel, 3, [(rows, LANES)] * 2, q, base), "gy")
 
     pairs, mode_pairs = pairs_of(vectors), pairs_of(modes)
@@ -554,7 +602,7 @@
     spaced = [spacing * n for n in range(modes * vectors)]
     advanced, planes, sums = call(
         functools.partial(advance_kernel, width, comps, 0, fields, 1),
-        8,
+        5,
         [(fields, rows, length), (2, fields, *plane), (modes * vectors, SUB, LANES)],
         q,
         base,
@@ -562,32 +610,37 @@
         *halo_y,
         direct,
     )
-    edge, payload = call(
-        functools.partial(edge_kernel, width, comps, (fields, fields), [spaced], 1, 0),
-        2,
-        [(2, fields, *plane), (devices, LANES)],
-        *layers,
-        *layers,
-        *halo_x,
-        *halo_x,
+    edge, payload = edges(
+        width,
+        comps,
+        (fields, fields),
+        spaced,
+        0.9,
+        devices,
+        layers,
+        layers,
+        halo_x,
+        halo_x,
         planes,
         sums,
-        direct_planes,
-    )
-    payload, late_a, late_b = lax.optimization_barrier((payload, late_a, late_b))
-    halo_late = swap(late_a, late_b, "gx")
+        [direct_planes],
+        [],
+    )
     gathered = exchange(payload)
 
     scratch = [pltpu.VMEM((modes * vectors, SUB, LANES), jnp.float32)]
-    layers = call(
-        functools.partial(deflate_planes_kernel, comps, spaced),
-        1.5,
-        [(fields, *plane)] * 2,
-        gathered,
-        edge,
-        dual_planes,
-        scratch=scratch,
-    )
+    layers = [
+        call(
+            functools.partial(deflate_planes_kernel, comps, spaced, side),
+            0.6,
+            [(fields, *plane)],
+            gathered,
+            edge[side],
+            dual_planes,
+            scratch=scratch,
+        )[0]
+        for side in range(2)
+    ]
     halo_x = swap(*layers, "gx")
     current, *columns = call(
         functools.partial(deflate_kernel, width, comps, spaced),
@@ -611,38 +664,40 @@
         direct,
         dual,
     )
-    lanes = [list(first.values()), list(cross.values()), list(self_gram.values())]
-    edge, payload = call(
-        functools.partial(edge_kernel, width, comps, (0, 0), lanes, 2, 1),
-        3,
-        [(2, fields, *plane), (devices, LANES)],
-        *layers,
-        late_a,
-        late_b,
-        *halo_x,
-        *halo_late,
+    lanes = list(first.values()) + list(cross.values()) + list(self_gram.values())
+    edge, payload = edges(
+        width,
+        comps,
+        (0, 0),
+        lanes,
+        1.3,
+        devices,
+        layers,
+        (late_a, late_b),
+        halo_x,
+        halo_late,
         planes,
         sums,
-        direct_planes,
-        dual_planes,
-        metric_part,
+        [direct_planes, dual_planes],
+        [metric_part],
     )
     total = exchange(payload)
     factor_count = vectors * (vectors + 1) // 2 + modes * vectors
+    chunks = math.gcd(rows // SUB, 4)
     next_block, growth = call(
         functools.partial(finish_kernel, width, comps, (first, cross, self_gram, metric), math.sqrt(cells)),
-        5,
+        3,
         [(fields, rows, length), (vectors, vectors)],
         total,
         dual,
         advanced,
-        edge,
+        *edge,
         scratch=[
             pltpu.VMEM((fields, rows, length), jnp.float32),
             pltpu.VMEM((factor_count, SUB, LANES), jnp.float32),
-            pltpu.SemaphoreType.DMA,
+            pltpu.SemaphoreType.DMA((chunks,)),
         ],
-        any_args=(2,),
+        hbm_outs=(0,),
     )
     return (next_block.reshape(adjoint_block.shape), growth)
 

time: 80 us -> 79.3 us (level)
  local copies, waits for them, and re-layouts: 6.97 us -> 1.9 us
  Pallas kernels: 26.6 us -> 29 us
  waiting for transfers between devices: 11.9 us -> 14 us
    unnamed x18 -> x6, local copies, waits for them, and re-layouts: 6.97 us -> 1.9 us
    pallas_call x10 -> x13, Pallas kernels: 26.6 us -> 29 us  [call(): pl.pallas_call(kernel, out_shape=[jax.ShapeDtypeStruct(shape, jnp.float32...]
    ppermute x10, waiting for transfers between devices: 11.9 us -> 14 us  [swap(): lax.ppermute(field, axis, pairs + [(j, i) for i, j in pairs])]
  transfers between devices with their start and end apart: 10 -> 10, of which waited for: 2 -> 2; matrix products, arithmetic and copies ran while one was open for 0% -> 0% of each run, Pallas kernels for 24% -> 26%
where the time goes in v2:
time: 79.3 us; the launch traced here: 79 us
  Pallas kernels  29 us (37%)
  blocking collectives  22.8 us (29%)
  waiting for transfers between devices  14 us (18%)
  starting transfers between devices  10.5 us (13%)
  local copies, waits for them, and re-layouts  1.9 us (2%)
  between operations  0.84 us (1%)
    pallas_call x13, Pallas kernels, call(): pl.pallas_call(kernel, out_shape=[jax.ShapeDtypeStruct(shape, jnp.float32...  29 us
    all_to_all x2, blocking collectives, exchange(): return lax.all_to_all(payload, ('gx', 'gy'), 0, 0, tiled=True)  22.8 us
    ppermute x10, waiting for transfers between devices, swap(): lax.ppermute(field, axis, pairs + [(j, i) for i, j in pairs])  14 us
    ppermute x10, starting transfers between devices, swap(): lax.ppermute(field, axis, pairs + [(j, i) for i, j in pairs])  10.5 us
    unnamed x6, local copies, waits for them, and re-layouts  1.9 us
  transfers between devices with their start and end apart: 10, of which 2 were waited for; matrix products, arithmetic and copies ran while one was open for 0% of the time, Pallas kernels for 26%

profile of v2, /device:TPU:0, one launch (start us, length us, event | category | flops | bytes accessed | tf_op | source)
XLA Modules:
  0.0 79.0 jit_solution(11862259081226261585)
XLA Ops:
  0.6 2.0 %shard_map.59 = (f32[12,256,128]{2,1,0:T(8,128)S(1)}, f32[6,256,128]{2,1,0:T(8,128)S(1)}, f32[15,64,128]{2,1,0:T(8,128)S(1)}, f32[15,64,128]{2,1,0:T(8,128)S(1)}...) custom-call(f32[12,256,128]{2,1,0:T(8,128)} %bitcast.26, f32[6,256,128]{2,1,0:T(8,128)} %bitcast.27), custom_call_target="tpu_custom_call" | custom-call | bytes 5250000 | tf_op jit(solution)/shard_map/pallas_call | solution.py:96
  2.6 3.0 %collective-permute-start.3 = (f32[15,64,128]{2,1,0:T(8,128)S(1)}, f32[15,64,128]{2,1,0:T(8,128)S(1)}, u32[]{:S(2)}, u32[]{:S(2)}) collective-permute-start(f32[15,64,128]{2,1,0:T(8,128)S(1)} %get-tuple-element.38.refs_0_.refs_1_), channel_id=1, source_target_pairs={{0,4},{8,12},{16,20},{24,28},{4,0},{12,8},{20,16},{28,24},{1,5},{9... | collective-permute-start | bytes 1474568 | tf_op jit(solution)/shard_map/ppermute | solution.py:546
  5.7 0.7 collective-permute-start
  6.4 1.8 %shard_map.60 = (f32[256,128]{1,0:T(8,128)S(1)}, f32[256,128]{1,0:T(8,128)S(1)}) custom-call(f32[12,256,128]{2,1,0:T(8,128)S(1)} %get-tuple-element.33.q_ref.refs_0_, f32[6,256,128]{2,1,0:T(8,128)S(1)} %get-tuple-element.34.base_ref.refs_1_), custom_call_target="tpu_custom_call" | custom-call | bytes 10500000 | tf_op jit(solution)/shard_map/pallas_call | solution.py:96
  8.1 0.1 collective-permute-start.1
  8.2 0.7 collective-permute-start.2
  8.9 0.0 copy-start.1
  8.9 1.9 %copy-done.1 = f32[8,3,64,4,128]{4,3,2,1,0:T(4,128)S(1)} copy-done((f32[8,3,64,4,128]{4,3,2,1,0:T(4,128)S(1)}, f32[8,3,64,4,128]{4,3,2,1,0:T(4,128)}, u32[]{:S(2)}) %copy-start.1) | copy-done | bytes 3145752
  10.8 2.2 %shard_map.62 = (f32[2,24,64,128]{3,2,1,0:T(8,128)S(1)}, f32[2,24,64,128]{3,2,1,0:T(8,128)S(1)}, f32[8,128]{1,0:T(8,128)S(1)}) custom-call(f32[24,256,128]{2,1,0:T(8,128)S(1)} %bitcast.17, f32[24,256,128]{2,1,0:T(8,128)S(1)} %bitcast.13), custom_call_target="tpu_custom_call" | custom-call | bytes 14000000 | tf_op jit(solution)/shard_map/pallas_call | solution.py:96
  13.0 0.0 collective-permute-done.1.refs_2_.refs_4_
  13.0 5.1 %shard_map.61 = (f32[12,256,128]{2,1,0:T(8,128)S(1)}, f32[2,12,64,128]{3,2,1,0:T(8,128)S(1)}, f32[32,8,128]{2,1,0:T(8,128)S(1)}) custom-call(f32[12,256,128]{2,1,0:T(8,128)S(1)} %get-tuple-element.33.q_ref.refs_0_, f32[6,256,128]{2,1,0:T(8,128)S(1)} %get-tuple-element.34.base_ref.refs_1_, f32[256,128]{1,0:T(8,128)S(1)} %collective-permute-done.1.refs_2_.refs_4_, ...), custom_call_target="tpu_custom_call" | custom-call | bytes 17500000 | tf_op jit(solution)/shard_map/pallas_call | solution.py:96
  18.1 8.5 %collective-permute-done.3.refs_2_.refs_3_ = f32[15,64,128]{2,1,0:T(8,128)S(1)} collective-permute-done((f32[15,64,128]{2,1,0:T(8,128)S(1)}, f32[15,64,128]{2,1,0:T(8,128)S(1)}, u32[]{:S(2)}, u32[]{:S(2)}) %collective-permute-start.3) | collective-permute-done | bytes 491552 | tf_op jit(solution)/shard_map/ppermute | solution.py:546
  26.7 0.6 shard_map.63
  27.2 1.1 %shard_map.64 = (f32[12,64,128]{2,1,0:T(8,128)S(1)}, f32[32,128]{1,0:T(8,128)S(1)}) custom-call(f32[15,64,128]{2,1,0:T(8,128)S(1)} %get-tuple-element.32.refs_0_.refs_1_, f32[15,64,128]{2,1,0:T(8,128)S(1)} %get-tuple-element.32.refs_0_.refs_1_, f32[15,64,128]{2,1,0:T(8,128)S(1)} %collective-permute-done.refs_2_.refs_3_, ...), custom_call_target="tpu_custom_call" | custom-call | bytes 3150000 | tf_op jit(solution)/shard_map/pallas_call | solution.py:96
  28.3 12.9 %all_to_all.22 = f32[32,1,128]{2,1,0:T(1,128)S(1)} all-to-all(f32[32,1,128]{2,1,0:T(1,128)S(1)} %bitcast.25), channel_id=1, replica_groups=mesh['gx'=8,'gy'=4] {'gx','gy'}, dimensions={0} | all-to-all | bytes 32768 | tf_op jit(solution)/shard_map/all_to_all | solution.py:551
  41.2 0.4 shard_map.66.planes_a.refs_0_
  41.7 0.6 collective-permute-start.8
  42.3 0.4 shard_map.65.planes_b.refs_0_
  42.8 0.7 collective-permute-start.4
  43.5 0.0 copy-start.2
  43.5 2.9 %shard_map.67 = (f32[12,256,128]{2,1,0:T(8,128)S(1)}, f32[256,128]{1,0:T(8,128)S(1)}, f32[256,128]{1,0:T(8,128)S(1)}) custom-call(f32[32,128]{1,0:T(8,128)S(1)} %bitcast.22, f32[12,256,128]{2,1,0:T(8,128)S(1)} %get-tuple-element.46.advanced, f32[24,256,128]{2,1,0:T(8,128)S(1)} %bitcast.14, f32[12,64,128]{2,1,0:T(8,128)S(1)} %shard_map.66.planes_a.refs_0_, ...), custom_call_target="tpu_custom_call" | custom-call | bytes 10500000 | tf_op jit(solution)/shard_map/pallas_call | solution.py:96
  46.4 0.1 collective-permute-start.6
  46.5 0.7 collective-permute-start.7
  47.1 3.3 %collective-permute-start.9 = (f32[3,64,128]{2,1,0:T(8,128)S(1)}, f32[3,64,128]{2,1,0:T(8,128)S(1)}, u32[]{:S(2)}, u32[]{:S(2)}) collective-permute-start(f32[3,64,128]{2,1,0:T(8,128)S(1)} %get-tuple-element.52.refs_1_), channel_id=1, source_target_pairs={{0,4},{8,12},{16,20},{24,28},{4,0},{12,8},{20,16},{28,24},{1,5},{9... | collective-permute-start | bytes 294920 | tf_op jit(solution)/shard_map/ppermute | solution.py:546
  50.5 0.7 collective-permute-start.5
  51.1 6.8 %shard_map.68 = (f32[12,256,128]{2,1,0:T(8,128)S(1)}, f32[2,12,64,128]{3,2,1,0:T(8,128)S(1)}, f32[74,8,128]{2,1,0:T(8,128)S(1)}) custom-call(f32[12,256,128]{2,1,0:T(8,128)S(1)} %get-tuple-element.48.refs_0_, f32[6,256,128]{2,1,0:T(8,128)S(1)} %get-tuple-element.34.base_ref.refs_1_, f32[256,128]{1,0:T(8,128)S(1)} %collective-permute-done.6.refs_2_, ...), custom_call_target="tpu_custom_call" | custom-call | bytes 42000000 | tf_op jit(solution)/shard_map/pallas_call | solution.py:96
  57.9 5.4 %collective-permute-done.9.refs_3_ = f32[3,64,128]{2,1,0:T(8,128)S(1)} collective-permute-done((f32[3,64,128]{2,1,0:T(8,128)S(1)}, f32[3,64,128]{2,1,0:T(8,128)S(1)}, u32[]{:S(2)}, u32[]{:S(2)}) %collective-permute-start.9) | collective-permute-done | bytes 98336 | tf_op jit(solution)/shard_map/ppermute | solution.py:546
  63.3 0.0 collective-permute-done.8.refs_2_
  63.3 0.9 %shard_map.69 = (f32[12,64,128]{2,1,0:T(8,128)S(1)}, f32[74,8,128]{2,1,0:T(8,128)S(1)}) custom-call(f32[12,64,128]{2,1,0:T(8,128)S(1)} %shard_map.66.planes_a.refs_0_, f32[3,64,128]{2,1,0:T(8,128)S(1)} %get-tuple-element.52.refs_1_, f32[12,64,128]{2,1,0:T(8,128)S(1)} %collective-permute-done.8.refs_2_, f32[3,64,128]{2,1,0:T(8,128)S(1)} %collective-permute-done.9.refs_3_, ...), custom_call_target="tpu_custom_call" | custom-call | bytes 4550000 | tf_op jit(solution)/shard_map/pallas_call | solution.py:96
  64.2 1.5 %shard_map.70 = (f32[12,64,128]{2,1,0:T(8,128)S(1)}, f32[32,128]{1,0:T(8,128)S(1)}) custom-call(f32[12,64,128]{2,1,0:T(8,128)S(1)} %shard_map.65.planes_b.refs_0_, f32[3,64,128]{2,1,0:T(8,128)S(1)} %get-tuple-element.45.refs_1_, f32[12,64,128]{2,1,0:T(8,128)S(1)} %collective-permute-done.4.refs_2_, f32[3,64,128]{2,1,0:T(8,128)S(1)} %collective-permute-done.5.refs_3_, ...), custom_call_target="tpu_custom_call" | custom-call | bytes 4550000 | tf_op jit(solution)/shard_map/pallas_call | solution.py:96
  65.7 9.9 %all_to_all.23 = f32[32,1,128]{2,1,0:T(1,128)S(1)} all-to-all(f32[32,1,128]{2,1,0:T(1,128)S(1)} %bitcast.24), channel_id=1, replica_groups=mesh['gx'=8,'gy'=4] {'gx','gy'}, dimensions={0} | all-to-all | bytes 32768 | tf_op jit(solution)/shard_map/all_to_all | solution.py:551
  75.6 3.4 %shard_map.71 = (f32[12,256,128]{2,1,0:T(8,128)}, f32[4,4]{1,0:T(4,128)}) custom-call(f32[32,128]{1,0:T(8,128)S(1)} %bitcast.23, f32[24,256,128]{2,1,0:T(8,128)S(1)} %bitcast.16, f32[12,256,128]{2,1,0:T(8,128)S(1)} %get-tuple-element.57.refs_2_, f32[12,64,128]{2,1,0:T(8,128)S(1)} %get-tuple-element.58.refs_3_, f32[12,64,128]{2,1,0:T(8,128)S(1)} %get-tuple-element.59.refs_4_), custom_call_target="tpu_custom_call" | custom-call | bytes 10500000 | tf_op jit(solution)/shard_map/pallas_call | solution.py:96
  (9 shorter events, 0.0 us)
Async XLA Ops:
  0.6 8.3 %copy-start = (f32[8,3,64,4,128]{4,3,2,1,0:T(4,128)S(1)}, f32[8,3,64,4,128]{4,3,2,1,0:T(4,128)}, u32[]{:S(2)}) copy-start(f32[8,3,64,4,128]{4,3,2,1,0:T(4,128)} %param.7) | copy-start | bytes 9437188
  2.6 24.0 %collective-permute-start.3 = (f32[15,64,128]{2,1,0:T(8,128)S(1)}, f32[15,64,128]{2,1,0:T(8,128)S(1)}, u32[]{:S(2)}, u32[]{:S(2)}) collective-permute-start(f32[15,64,128]{2,1,0:T(8,128)S(1)} %get-tuple-element.38.refs_0_.refs_1_), channel_id=1, source_target_pairs={{0,4},{8,12},{16,20},{24,28},{4,0},{12,8},{20,16},{28,24},{1,5},{9... | collective-permute-start | bytes 1474568 | tf_op jit(solution)/shard_map/ppermute | solution.py:546
  5.7 21.6 %collective-permute-start = (f32[15,64,128]{2,1,0:T(8,128)S(1)}, f32[15,64,128]{2,1,0:T(8,128)S(1)}, u32[]{:S(2)}, u32[]{:S(2)}) collective-permute-start(f32[15,64,128]{2,1,0:T(8,128)S(1)} %get-tuple-element.32.refs_0_.refs_1_), channel_id=1, source_target_pairs={{4,8},{12,16},{20,24},{8,4},{16,12},{24,20},{5,9},{13,17},{21,25},... | collective-permute-start | bytes 1474568 | tf_op jit(solution)/shard_map/ppermute | solution.py:546
  8.1 4.9 %collective-permute-start.1 = (f32[256,128]{1,0:T(8,128)S(1)}, f32[256,128]{1,0:T(8,128)S(1)}, u32[]{:S(2)}, u32[]{:S(2)}) collective-permute-start(f32[256,128]{1,0:T(8,128)S(1)} %get-tuple-element.35), channel_id=1, source_target_pairs={{0,1},{2,3},{1,0},{3,2},{4,5},{6,7},{5,4},{7,6},{8,9},{10,11},{9,8... | collective-permute-start | bytes 393224 | tf_op jit(solution)/shard_map/ppermute | solution.py:546
  8.2 4.8 %collective-permute-start.2 = (f32[256,128]{1,0:T(8,128)S(1)}, f32[256,128]{1,0:T(8,128)S(1)}, u32[]{:S(2)}, u32[]{:S(2)}) collective-permute-start(f32[256,128]{1,0:T(8,128)S(1)} %get-tuple-element.36), channel_id=1, source_target_pairs={{1,2},{2,1},{5,6},{6,5},{9,10},{10,9},{13,14},{14,13},{17,18},{18,... | collective-permute-start | bytes 393224 | tf_op jit(solution)/shard_map/ppermute | solution.py:546
  8.9 1.9 %copy-start.1 = (f32[8,3,64,4,128]{4,3,2,1,0:T(4,128)S(1)}, f32[8,3,64,4,128]{4,3,2,1,0:T(4,128)}, u32[]{:S(2)}) copy-start(f32[8,3,64,4,128]{4,3,2,1,0:T(4,128)} %param.6) | copy-start | bytes 9437188
  41.7 21.6 %collective-permute-start.8 = (f32[12,64,128]{2,1,0:T(8,128)S(1)}, f32[12,64,128]{2,1,0:T(8,128)S(1)}, u32[]{:S(2)}, u32[]{:S(2)}) collective-permute-start(f32[12,64,128]{2,1,0:T(8,128)S(1)} %shard_map.66.planes_a.refs_0_), channel_id=1, source_target_pairs={{0,4},{8,12},{16,20},{24,28},{4,0},{12,8},{20,16},{28,24},{1,5},{9... | collective-permute-start | bytes 1179656 | tf_op jit(solution)/shard_map/ppermute | solution.py:546
  42.8 21.4 %collective-permute-start.4 = (f32[12,64,128]{2,1,0:T(8,128)S(1)}, f32[12,64,128]{2,1,0:T(8,128)S(1)}, u32[]{:S(2)}, u32[]{:S(2)}) collective-permute-start(f32[12,64,128]{2,1,0:T(8,128)S(1)} %shard_map.65.planes_b.refs_0_), channel_id=1, source_target_pairs={{4,8},{12,16},{20,24},{8,4},{16,12},{24,20},{5,9},{13,17},{21,25},... | collective-permute-start | bytes 1179656 | tf_op jit(solution)/shard_map/ppermute | solution.py:546
  43.5 7.7 %copy-start.2 = (f32[8,3,64,4,128]{4,3,2,1,0:T(4,128)S(1)}, f32[8,3,64,4,128]{4,3,2,1,0:T(4,128)}, u32[]{:S(2)}) copy-start(f32[8,3,64,4,128]{4,3,2,1,0:T(4,128)} %param.6) | copy-start | bytes 9437188
  46.4 4.1 %collective-permute-start.6 = (f32[256,128]{1,0:T(8,128)S(1)}, f32[256,128]{1,0:T(8,128)S(1)}, u32[]{:S(2)}, u32[]{:S(2)}) collective-permute-start(f32[256,128]{1,0:T(8,128)S(1)} %get-tuple-element.49), channel_id=1, source_target_pairs={{0,1},{2,3},{1,0},{3,2},{4,5},{6,7},{5,4},{7,6},{8,9},{10,11},{9,8... | collective-permute-start | bytes 393224 | tf_op jit(solution)/shard_map/ppermute | solution.py:546
  46.5 4.7 %collective-permute-start.7 = (f32[256,128]{1,0:T(8,128)S(1)}, f32[256,128]{1,0:T(8,128)S(1)}, u32[]{:S(2)}, u32[]{:S(2)}) collective-permute-start(f32[256,128]{1,0:T(8,128)S(1)} %get-tuple-element.50), channel_id=1, source_target_pairs={{1,2},{2,1},{5,6},{6,5},{9,10},{10,9},{13,14},{14,13},{17,18},{18,... | collective-permute-start | bytes 393224 | tf_op jit(solution)/shard_map/ppermute | solution.py:546
  47.1 16.2 %collective-permute-start.9 = (f32[3,64,128]{2,1,0:T(8,128)S(1)}, f32[3,64,128]{2,1,0:T(8,128)S(1)}, u32[]{:S(2)}, u32[]{:S(2)}) collective-permute-start(f32[3,64,128]{2,1,0:T(8,128)S(1)} %get-tuple-element.52.refs_1_), channel_id=1, source_target_pairs={{0,4},{8,12},{16,20},{24,28},{4,0},{12,8},{20,16},{28,24},{1,5},{9... | collective-permute-start | bytes 294920 | tf_op jit(solution)/shard_map/ppermute | solution.py:546
  50.5 13.7 %collective-permute-start.5 = (f32[3,64,128]{2,1,0:T(8,128)S(1)}, f32[3,64,128]{2,1,0:T(8,128)S(1)}, u32[]{:S(2)}, u32[]{:S(2)}) collective-permute-start(f32[3,64,128]{2,1,0:T(8,128)S(1)} %get-tuple-element.45.refs_1_), channel_id=1, source_target_pairs={{4,8},{12,16},{20,24},{8,4},{16,12},{24,20},{5,9},{13,17},{21,25},... | collective-permute-start | bytes 294920 | tf_op jit(solution)/shard_map/ppermute | solution.py:546

commit v3 on v2

--- a/solution.py
+++ b/solution.py
@@ -158,12 +158,21 @@
     pack_y(fields, first_ref, second_ref, q_ref.shape[1] // SUB)
 
 
-def modes_kernel(width, modes, slot, direct_ref, dual_ref, direct_planes, dual_planes, metric_ref):
+def modes_kernel(
+    width, modes, slot, direct_hbm, dual_hbm, direct_ref, dual_ref, direct_planes, dual_planes, metric_ref, semaphore
+):
     depth = direct_planes.shape[2]
     comps = direct_ref.shape[0] // modes
     layers, _ = sides(width)
-    for ref, planes in ((direct_ref, direct_planes), (dual_ref, dual_planes)):
-        for f in range(ref.shape[0]):
+    parts = ((dual_hbm, dual_ref, dual_planes), (direct_hbm, direct_ref, direct_planes))
+    copies = []
+    for n, (source, ref, _) in enumerate(parts):
+        for f in range(modes * comps):
+            copies.append(pltpu.make_async_copy(source.at[f], ref.at[f], semaphore.at[n, f]))
+            copies[-1].start()
+    for n, (_, ref, planes) in enumerate(parts):
+        for f in range(modes * comps):
+            copies[n * modes * comps + f].wait()
             for side, x in enumerate(layers):
                 planes[side, f] = ref[f, pl.ds(x, depth, stride=width), :]
     todo = pairs_of(modes)
@@ -197,6 +206,7 @@
     x_at = row % width
     low_x = jnp.where(x_at > 0, 1.0, 0.0)
     high_x = jnp.where(x_at < width - 1, 1.0, 0.0)
+    upper = row < width
 
     def around(ref, f, k, before, after, halo, lane_at):
         here = block(ref, f, k)
@@ -295,25 +305,29 @@
             at += 1
 
 
-def edge_kernel(width, comps, side, at, lanes, projections, extra, *refs):
-    own_q, own_b, halo_q, halo_b, advanced, sums_ref = refs[:6]
-    mode_refs, refs = refs[6 : 6 + projections], refs[6 + projections :]
-    extra_refs, (new_ref, result_ref) = refs[:extra], refs[extra:]
-    fields, depth = new_ref.shape[:2]
+def edge_kernel(width, comps, at, lanes, projections, extra, *refs):
+    own_q, own_b, halo_q, halo_b = (refs[n : n + 2] for n in (0, 2, 4, 6))
+    advanced, sums_ref = refs[8:10]
+    mode_refs, refs = refs[10 : 10 + projections], refs[10 + projections :]
+    extra_refs, (new_a, new_b, payload_ref) = refs[:extra], refs[extra:]
+    new_refs = (new_a, new_b)
+    fields, depth = new_a.shape[:2]
     vectors, blocks = fields // comps, depth // SUB
-    scale = sides(width)[1][side] * HALF
+    _, signs = sides(width)
 
     def step(k, carry):
         rows = pl.ds(pl.multiple_of(k * SUB, SUB), SUB)
-        factor = DIFF + scale * own_b[at[0], rows, :]
-        outer = [scale * halo_b[at[1] + j, rows, :] for j in range(comps)]
-        for v in range(vectors):
-            for c in range(comps):
-                value = factor * halo_q[v * comps + c, rows, :]
-                if c == 0:
-                    for j in range(comps):
-                        value = value - own_q[v * comps + j, rows, :] * outer[j]
-                new_ref[v * comps + c, rows, :] = value
+        for side in range(2):
+            scale = signs[side] * HALF
+            factor = DIFF + scale * own_b[side][at[0], rows, :]
+            outer = [scale * halo_b[side][at[1] + j, rows, :] for j in range(comps)]
+            for v in range(vectors):
+                for c in range(comps):
+                    value = factor * halo_q[side][v * comps + c, rows, :]
+                    if c == 0:
+                        for j in range(comps):
+                            value = value - own_q[side][v * comps + j, rows, :] * outer[j]
+                    new_refs[side][v * comps + c, rows, :] = value
         return carry
 
     lax.fori_loop(0, blocks, step, 0)
@@ -325,12 +339,13 @@
         def dots(k, accs, ref=ref):
             accs = list(accs)
             rows = pl.ds(pl.multiple_of(k * SUB, SUB), SUB)
-            for c in range(comps):
-                right = [new_ref[v * comps + c, rows, :] for v in range(vectors)]
-                for m in range(modes):
-                    left = ref[side, m * comps + c, rows, :]
-                    for v in range(vectors):
-                        accs[m * vectors + v] = accs[m * vectors + v] + left * right[v]
+            for side in range(2):
+                for c in range(comps):
+                    right = [new_refs[side][v * comps + c, rows, :] for v in range(vectors)]
+                    for m in range(modes):
+                        left = ref[side, m * comps + c, rows, :]
+                        for v in range(vectors):
+                            accs[m * vectors + v] = accs[m * vectors + v] + left * right[v]
             return tuple(accs)
 
         total += lax.fori_loop(0, blocks, dots, accs)
@@ -341,22 +356,19 @@
     def finish(k, accs):
         accs = list(accs)
         rows = pl.ds(pl.multiple_of(k * SUB, SUB), SUB)
-        for c in range(comps):
-            inner = []
-            for v in range(vectors):
-                f = v * comps + c
-                inner.append(new_ref[f, rows, :] + advanced[side, f, rows, :])
-                new_ref[f, rows, :] = inner[v]
-            if squares:
-                for n, (i, j) in enumerate(own):
-                    accs[n] = accs[n] + inner[i] * inner[j]
+        for side in range(2):
+            for c in range(comps):
+                inner = []
+                for v in range(vectors):
+                    f = v * comps + c
+                    inner.append(new_refs[side][f, rows, :] + advanced[side, f, rows, :])
+                    new_refs[side][f, rows, :] = inner[v]
+                if squares:
+                    for n, (i, j) in enumerate(own):
+                        accs[n] = accs[n] + inner[i] * inner[j]
         return tuple(accs)
 
     total += lax.fori_loop(0, blocks, finish, accs)
-    if lanes is None:
-        for n, value in enumerate(total):
-            result_ref[n] = value
-        return
     slots = dict(zip(lanes, total))
     lane = lane_ids()
     inside = lane < 0
@@ -365,52 +377,40 @@
     packed = jnp.where(inside, lane_sums([slots.get(i) for i in range(LANES)]), 0.0)
     for ref in extra_refs:
         packed = packed + ref[...]
-    for first in range(0, result_ref.shape[0], SUB):
-        result_ref[first : first + SUB, :] = packed
+    for first in range(0, payload_ref.shape[0], SUB):
+        payload_ref[first : first + SUB, :] = packed
 
 
 def edges(width, comps, at, lanes, micros, devices, own_q, own_b, halo_q, halo_b, advanced, sums, modes, extra):
-    layers = []
-    for side in range(2):
-        last = side == 1
-        kernel = functools.partial(
-            edge_kernel, width, comps, side, at, lanes if last else None, len(modes), len(extra) if last else 0
-        )
-        new, sums = call(
-            kernel,
-            micros,
-            [advanced.shape[1:], (devices, LANES) if last else sums.shape],
-            own_q[side],
-            own_b[side],
-            halo_q[side],
-            halo_b[side],
-            advanced,
-            sums,
-            *modes,
-            *(extra if last else ()),
-        )
-        layers.append(new)
-    return layers, sums
-
-
-def deflate_planes_kernel(comps, lanes, side, gathered, planes, dual_planes, out, factors):
+    kernel = functools.partial(edge_kernel, width, comps, at, lanes, len(modes), len(extra))
+    shapes = [advanced.shape[1:], advanced.shape[1:], (devices, LANES)]
+    args = (*own_q, *own_b, *halo_q, *halo_b, advanced, sums, *modes, *extra)
+    *layers, payload = call(kernel, micros, shapes, *args)
+    return layers, payload
+
+
+def deflate_planes_kernel(comps, lanes, gathered, plane_a, plane_b, late_a, late_b, dual_planes, out_a, out_b, factors):
     total = gathered_total(gathered)
     for i, lane in enumerate(lanes):
         factors[i] = spread(total, lane)
-    fields, depth = out.shape[:2]
+    fields, depth = plane_a.shape[:2]
     vectors = fields // comps
     modes = dual_planes.shape[1] // comps
+    for late, out in ((late_a, out_a), (late_b, out_b)):
+        for j in range(comps):
+            out[fields + j] = late[j]
 
     def step(k, carry):
         rows = pl.ds(pl.multiple_of(k * SUB, SUB), SUB)
-        for c in range(comps):
-            values = [planes[v * comps + c, rows, :] for v in range(vectors)]
-            for m in range(modes):
-                mode = dual_planes[side, m * comps + c, rows, :]
+        for side, (plane, out) in enumerate(((plane_a, out_a), (plane_b, out_b))):
+            for c in range(comps):
+                values = [plane[v * comps + c, rows, :] for v in range(vectors)]
+                for m in range(modes):
+                    mode = dual_planes[side, m * comps + c, rows, :]
+                    for v in range(vectors):
+                        values[v] = values[v] - factors[m * vectors + v] * mode
                 for v in range(vectors):
-                    values[v] = values[v] - factors[m * vectors + v] * mode
-            for v in range(vectors):
-                out[v * comps + c, rows, :] = values[v]
+                    out[v * comps + c, rows, :] = values[v]
         return carry
 
     lax.fori_loop(0, depth // SUB, step, 0)
@@ -447,7 +447,7 @@
 
 
 def finish_kernel(width, comps, layout, scale, *refs):
-    gathered, dual, advanced, *planes, out_hbm, growth_ref, out_ref, factors, semaphore = refs
+    gathered, dual, advanced, *planes, out_hbm, growth_hbm, out_ref, growth_ref, factors, semaphore = refs
     fields, rows_all = out_ref.shape[:2]
     vectors, modes = fields // comps, dual.shape[0] // comps
     depth = rows_all // width
@@ -491,6 +491,9 @@
     for (i, j), value in lower.items():
         growth = jnp.where((row == i) & (lane == j), value, growth)
     growth_ref[...] = growth[:vectors, :vectors]
+    chunks = semaphore.shape[0] - 1
+    copies = [pltpu.make_async_copy(growth_ref, growth_hbm, semaphore.at[chunks])]
+    copies[0].start()
     at = {}
     for (i, j), value in inverse.items():
         at[i, j] = len(at)
@@ -525,9 +528,7 @@
                 put_block(out_ref, i * comps + c, k, values[i])
         return carry
 
-    chunks = semaphore.shape[0]
     size = rows_all // SUB // chunks
-    copies = []
     for n in range(chunks):
         lax.fori_loop(n * size, (n + 1) * size, step, 0)
         rows = pl.ds(n * size * SUB, size * SUB)
@@ -580,7 +581,6 @@
         hbm_args=(0, 1),
     )
     halo_x = swap(*layers, "gx")
-    halo_late = swap(late_a, late_b, "gx")
     halo_y = swap(*call(pack_y_kernel, 3, [(rows, LANES)] * 2, q, base), "gy")
 
     pairs, mode_pairs = pairs_of(vectors), pairs_of(modes)
@@ -590,12 +590,14 @@
     slot = 2 * modes * vectors + len(pairs)
     metric = {key: slot + n for n, key in enumerate(mode_pairs)}
     assert slot + len(mode_pairs) <= LANES
-    direct_planes, dual_planes, metric_part = call(
+    direct, dual, direct_planes, dual_planes, metric_part = call(
         functools.partial(modes_kernel, width, modes, slot),
         4,
-        [(2, modes * comps, *plane)] * 2 + [(SUB, LANES)],
+        [direct.shape, dual.shape] + [(2, modes * comps, *plane)] * 2 + [(SUB, LANES)],
         direct,
         dual,
+        scratch=[pltpu.SemaphoreType.DMA((2, modes * comps))],
+        hbm_args=(0, 1),
     )
 
     spacing = LANES // (1 << (modes * vectors - 1).bit_length())
@@ -615,7 +617,7 @@
         comps,
         (fields, fields),
         spaced,
-        0.9,
+        1.5,
         devices,
         layers,
         layers,
@@ -629,18 +631,17 @@
     gathered = exchange(payload)
 
     scratch = [pltpu.VMEM((modes * vectors, SUB, LANES), jnp.float32)]
-    layers = [
-        call(
-            functools.partial(deflate_planes_kernel, comps, spaced, side),
-            0.6,
-            [(fields, *plane)],
-            gathered,
-            edge[side],
-            dual_planes,
-            scratch=scratch,
-        )[0]
-        for side in range(2)
-    ]
+    layers = call(
+        functools.partial(deflate_planes_kernel, comps, spaced),
+        0.8,
+        [(fields + comps, *plane)] * 2,
+        gathered,
+        *edge,
+        late_a,
+        late_b,
+        dual_planes,
+        scratch=scratch,
+    )
     halo_x = swap(*layers, "gx")
     current, *columns = call(
         functools.partial(deflate_kernel, width, comps, spaced),
@@ -668,14 +669,14 @@
     edge, payload = edges(
         width,
         comps,
-        (0, 0),
+        (fields, fields),
         lanes,
-        1.3,
+        2.2,
         devices,
         layers,
-        (late_a, late_b),
+        layers,
         halo_x,
-        halo_late,
+        halo_x,
         planes,
         sums,
         [direct_planes, dual_planes],
@@ -683,7 +684,7 @@
     )
     total = exchange(payload)
     factor_count = vectors * (vectors + 1) // 2 + modes * vectors
-    chunks = math.gcd(rows // SUB, 4)
+    chunks = math.gcd(rows // SUB, 8)
     next_block, growth = call(
         functools.partial(finish_kernel, width, comps, (first, cross, self_gram, metric), math.sqrt(cells)),
         3,
@@ -694,10 +695,11 @@
         *edge,
         scratch=[
             pltpu.VMEM((fields, rows, length), jnp.float32),
+            pltpu.VMEM((vectors, vectors), jnp.float32),
             pltpu.VMEM((factor_count, SUB, LANES), jnp.float32),
-            pltpu.SemaphoreType.DMA((chunks,)),
+            pltpu.SemaphoreType.DMA((chunks + 1,)),
         ],
-        hbm_outs=(0,),
+        hbm_outs=(0, 1),
     )
     return (next_block.reshape(adjoint_block.shape), growth)
 

time: 79.3 us -> 78.3 us (0.987)
  starting transfers between devices: 10.5 us -> 6.5 us
  waiting for transfers between devices: 14 us -> 17.4 us
  local copies, waits for them, and re-layouts: 1.9 us -> 0 us
  Pallas kernels: 29 us -> 30.6 us
    ppermute x10 -> x8, starting transfers between devices: 10.5 us -> 6.5 us  [swap(): lax.ppermute(field, axis, pairs + [(j, i) for i, j in pairs])]
    ppermute x10 -> x8, waiting for transfers between devices: 14 us -> 17.4 us  [swap(): lax.ppermute(field, axis, pairs + [(j, i) for i, j in pairs])]
    unnamed x6 -> x0, local copies, waits for them, and re-layouts: 1.9 us -> none
    pallas_call x13 -> x10, Pallas kernels: 29 us -> 30.6 us  [call(): pl.pallas_call(kernel, out_shape=[jax.ShapeDtypeStruct(shape, jnp.float32...]
  transfers between devices with their start and end apart: 10 -> 8, of which waited for: 2 -> 3; matrix products, arithmetic and copies ran while one was open for 0% -> 0% of each run, Pallas kernels for 26% -> 28%
where the time goes in v3:
time: 78.3 us; the launch traced here: 78.1 us
  Pallas kernels  30.6 us (39%)
  blocking collectives  22.8 us (29%)
  waiting for transfers between devices  17.4 us (22%)
  starting transfers between devices  6.5 us (8%)
    pallas_call x10, Pallas kernels, call(): pl.pallas_call(kernel, out_shape=[jax.ShapeDtypeStruct(shape, jnp.float32...  30.6 us
    all_to_all x2, blocking collectives, exchange(): return lax.all_to_all(payload, ('gx', 'gy'), 0, 0, tiled=True)  22.8 us
    ppermute x8, waiting for transfers between devices, swap(): lax.ppermute(field, axis, pairs + [(j, i) for i, j in pairs])  17.4 us
    ppermute x8, starting transfers between devices, swap(): lax.ppermute(field, axis, pairs + [(j, i) for i, j in pairs])  6.5 us
  transfers between devices with their start and end apart: 8, of which 3 were waited for; matrix products, arithmetic and copies ran while one was open for 0% of the time, Pallas kernels for 28%

profile of v3, /device:TPU:0, one launch (start us, length us, event | category | flops | bytes accessed | tf_op | source)
XLA Modules:
  0.0 78.1 jit_solution(9686293093550206382)
XLA Ops:
  0.6 1.8 %shard_map.59 = (f32[12,256,128]{2,1,0:T(8,128)S(1)}, f32[6,256,128]{2,1,0:T(8,128)S(1)}, f32[15,64,128]{2,1,0:T(8,128)S(1)}, f32[15,64,128]{2,1,0:T(8,128)S(1)}...) custom-call(f32[12,256,128]{2,1,0:T(8,128)} %bitcast.20, f32[6,256,128]{2,1,0:T(8,128)} %bitcast.21), custom_call_target="tpu_custom_call" | custom-call | bytes 5250000 | tf_op jit(solution)/shard_map/pallas_call | solution.py:96
  2.5 3.0 %collective-permute-start = (f32[15,64,128]{2,1,0:T(8,128)S(1)}, f32[15,64,128]{2,1,0:T(8,128)S(1)}, u32[]{:S(2)}, u32[]{:S(2)}) collective-permute-start(f32[15,64,128]{2,1,0:T(8,128)S(1)} %get-tuple-element.34.refs_0_.refs_2_), channel_id=1, source_target_pairs={{0,4},{8,12},{16,20},{24,28},{4,0},{12,8},{20,16},{28,24},{1,5},{9... | collective-permute-start | bytes 1474568 | tf_op jit(solution)/shard_map/ppermute | solution.py:547
  5.5 0.7 collective-permute-start.1
  6.2 1.8 %shard_map.60 = (f32[256,128]{1,0:T(8,128)S(1)}, f32[256,128]{1,0:T(8,128)S(1)}) custom-call(f32[12,256,128]{2,1,0:T(8,128)S(1)} %get-tuple-element.36.q_ref.refs_0_, f32[6,256,128]{2,1,0:T(8,128)S(1)} %get-tuple-element.37.base_ref.refs_1_), custom_call_target="tpu_custom_call" | custom-call | bytes 10500000 | tf_op jit(solution)/shard_map/pallas_call | solution.py:96
  8.0 0.1 collective-permute-start.2
  8.1 0.7 collective-permute-start.3
  8.7 5.1 %shard_map.61 = (f32[24,256,128]{2,1,0:T(8,128)S(1)}, f32[24,256,128]{2,1,0:T(8,128)S(1)}, f32[2,24,64,128]{3,2,1,0:T(8,128)S(1)}, f32[2,24,64,128]{3,2,1,0:T(8,128)S(1)}, f32[8,128]{1,0:T(8,128)S(1)}) custom-call(f32[24,256,128]{2,1,0:T(8,128)} %bitcast.18, f32[24,256,128]{2,1,0:T(8,128)} %bitcast.19), custom_call_target="tpu_custom_call" | custom-call | bytes 14000000 | tf_op jit(solution)/shard_map/pallas_call | solution.py:96
  13.8 0.0 collective-permute-done.2.refs_2_.refs_4_
  13.8 0.0 collective-permute-done.3.refs_3_.refs_5_
  13.8 5.1 %shard_map.62 = (f32[12,256,128]{2,1,0:T(8,128)S(1)}, f32[2,12,64,128]{3,2,1,0:T(8,128)S(1)}, f32[32,8,128]{2,1,0:T(8,128)S(1)}) custom-call(f32[12,256,128]{2,1,0:T(8,128)S(1)} %get-tuple-element.36.q_ref.refs_0_, f32[6,256,128]{2,1,0:T(8,128)S(1)} %get-tuple-element.37.base_ref.refs_1_, f32[256,128]{1,0:T(8,128)S(1)} %collective-permute-done.2.refs_2_.refs_4_, ...), custom_call_target="tpu_custom_call" | custom-call | bytes 17500000 | tf_op jit(solution)/shard_map/pallas_call | solution.py:96
  19.0 7.5 %collective-permute-done.refs_4_.refs_6_ = f32[15,64,128]{2,1,0:T(8,128)S(1)} collective-permute-done((f32[15,64,128]{2,1,0:T(8,128)S(1)}, f32[15,64,128]{2,1,0:T(8,128)S(1)}, u32[]{:S(2)}, u32[]{:S(2)}) %collective-permute-start) | collective-permute-done | bytes 491552 | tf_op jit(solution)/shard_map/ppermute | solution.py:547
  26.5 0.0 collective-permute-done.1.refs_5_.refs_7_
  26.5 1.6 %shard_map.63 = (f32[12,64,128]{2,1,0:T(8,128)S(1)}, f32[12,64,128]{2,1,0:T(8,128)S(1)}, f32[32,128]{1,0:T(8,128)S(1)}) custom-call(f32[15,64,128]{2,1,0:T(8,128)S(1)} %get-tuple-element.34.refs_0_.refs_2_, f32[15,64,128]{2,1,0:T(8,128)S(1)} %get-tuple-element.35.refs_1_.refs_3_, f32[15,64,128]{2,1,0:T(8,128)S(1)} %get-tuple-element.34.refs_0_.refs_2_, ...), custom_call_target="tpu_custom_call" | custom-call | bytes 5250000 | tf_op jit(solution)/shard_map/pallas_call | solution.py:96
  28.1 12.9 %all_to_all.22 = f32[32,1,128]{2,1,0:T(1,128)S(1)} all-to-all(f32[32,1,128]{2,1,0:T(1,128)S(1)} %bitcast.17), channel_id=1, replica_groups=mesh['gx'=8,'gy'=4] {'gx','gy'}, dimensions={0} | all-to-all | bytes 32768 | tf_op jit(solution)/shard_map/all_to_all | solution.py:552
  41.0 0.7 shard_map.64
  41.7 0.6 collective-permute-start.4
  42.3 0.7 collective-permute-start.5
  43.0 2.9 %shard_map.65 = (f32[12,256,128]{2,1,0:T(8,128)S(1)}, f32[256,128]{1,0:T(8,128)S(1)}, f32[256,128]{1,0:T(8,128)S(1)}) custom-call(f32[32,128]{1,0:T(8,128)S(1)} %bitcast.14, f32[12,256,128]{2,1,0:T(8,128)S(1)} %get-tuple-element.52.advanced, f32[24,256,128]{2,1,0:T(8,128)S(1)} %get-tuple-element.53.dual.refs_7_.refs_1_, ...), custom_call_target="tpu_custom_call" | custom-call | bytes 10500000 | tf_op jit(solution)/shard_map/pallas_call | solution.py:96
  45.9 0.1 collective-permute-start.6
  46.0 0.7 collective-permute-start.7
  46.7 0.7 collective-permute-done.6.refs_2_
  47.3 0.0 collective-permute-done.7.refs_3_
  47.3 6.8 %shard_map.66 = (f32[12,256,128]{2,1,0:T(8,128)S(1)}, f32[2,12,64,128]{3,2,1,0:T(8,128)S(1)}, f32[74,8,128]{2,1,0:T(8,128)S(1)}) custom-call(f32[12,256,128]{2,1,0:T(8,128)S(1)} %get-tuple-element.54.refs_0_, f32[6,256,128]{2,1,0:T(8,128)S(1)} %get-tuple-element.37.base_ref.refs_1_, f32[256,128]{1,0:T(8,128)S(1)} %collective-permute-done.6.refs_2_, ...), custom_call_target="tpu_custom_call" | custom-call | bytes 42000000 | tf_op jit(solution)/shard_map/pallas_call | solution.py:96
  54.1 9.2 %collective-permute-done.4.refs_4_.refs_6_ = f32[15,64,128]{2,1,0:T(8,128)S(1)} collective-permute-done((f32[15,64,128]{2,1,0:T(8,128)S(1)}, f32[15,64,128]{2,1,0:T(8,128)S(1)}, u32[]{:S(2)}, u32[]{:S(2)}) %collective-permute-start.4) | collective-permute-done | bytes 491552 | tf_op jit(solution)/shard_map/ppermute | solution.py:547
  63.3 0.0 collective-permute-done.5.refs_5_.refs_7_
  63.3 2.1 %shard_map.67 = (f32[12,64,128]{2,1,0:T(8,128)S(1)}, f32[12,64,128]{2,1,0:T(8,128)S(1)}, f32[32,128]{1,0:T(8,128)S(1)}) custom-call(f32[15,64,128]{2,1,0:T(8,128)S(1)} %get-tuple-element.50.planes_a.refs_0_.refs_2_, f32[15,64,128]{2,1,0:T(8,128)S(1)} %get-tuple-element.51.planes_b.refs_1_.refs_3_, ...), custom_call_target="tpu_custom_call" | custom-call | bytes 7700000 | tf_op jit(solution)/shard_map/pallas_call | solution.py:96
  65.4 9.9 %all_to_all.23 = f32[32,1,128]{2,1,0:T(1,128)S(1)} all-to-all(f32[32,1,128]{2,1,0:T(1,128)S(1)} %bitcast.16), channel_id=1, replica_groups=mesh['gx'=8,'gy'=4] {'gx','gy'}, dimensions={0} | all-to-all | bytes 32768 | tf_op jit(solution)/shard_map/all_to_all | solution.py:552
  75.3 2.8 %shard_map.68 = (f32[12,256,128]{2,1,0:T(8,128)}, f32[4,4]{1,0:T(4,128)}) custom-call(f32[32,128]{1,0:T(8,128)S(1)} %bitcast.15, f32[24,256,128]{2,1,0:T(8,128)S(1)} %get-tuple-element.53.dual.refs_7_.refs_1_, f32[12,256,128]{2,1,0:T(8,128)S(1)} %get-tuple-element.61.refs_2_, f32[12,64,128]{2,1,0:T(8,128)S(1)} %get-tuple-element.62.refs_3_, ...), custom_call_target="tpu_custom_call" | custom-call | bytes 10500000 | tf_op jit(solution)/shard_map/pallas_call | solution.py:96
Async XLA Ops:
  2.5 24.0 %collective-permute-start = (f32[15,64,128]{2,1,0:T(8,128)S(1)}, f32[15,64,128]{2,1,0:T(8,128)S(1)}, u32[]{:S(2)}, u32[]{:S(2)}) collective-permute-start(f32[15,64,128]{2,1,0:T(8,128)S(1)} %get-tuple-element.34.refs_0_.refs_2_), channel_id=1, source_target_pairs={{0,4},{8,12},{16,20},{24,28},{4,0},{12,8},{20,16},{28,24},{1,5},{9... | collective-permute-start | bytes 1474568 | tf_op jit(solution)/shard_map/ppermute | solution.py:547
  5.5 21.0 %collective-permute-start.1 = (f32[15,64,128]{2,1,0:T(8,128)S(1)}, f32[15,64,128]{2,1,0:T(8,128)S(1)}, u32[]{:S(2)}, u32[]{:S(2)}) collective-permute-start(f32[15,64,128]{2,1,0:T(8,128)S(1)} %get-tuple-element.35.refs_1_.refs_3_), channel_id=1, source_target_pairs={{4,8},{12,16},{20,24},{8,4},{16,12},{24,20},{5,9},{13,17},{21,25},... | collective-permute-start | bytes 1474568 | tf_op jit(solution)/shard_map/ppermute | solution.py:547
  8.0 5.8 %collective-permute-start.2 = (f32[256,128]{1,0:T(8,128)S(1)}, f32[256,128]{1,0:T(8,128)S(1)}, u32[]{:S(2)}, u32[]{:S(2)}) collective-permute-start(f32[256,128]{1,0:T(8,128)S(1)} %get-tuple-element.38), channel_id=1, source_target_pairs={{0,1},{2,3},{1,0},{3,2},{4,5},{6,7},{5,4},{7,6},{8,9},{10,11},{9,8... | collective-permute-start | bytes 393224 | tf_op jit(solution)/shard_map/ppermute | solution.py:547
  8.1 5.8 %collective-permute-start.3 = (f32[256,128]{1,0:T(8,128)S(1)}, f32[256,128]{1,0:T(8,128)S(1)}, u32[]{:S(2)}, u32[]{:S(2)}) collective-permute-start(f32[256,128]{1,0:T(8,128)S(1)} %get-tuple-element.39), channel_id=1, source_target_pairs={{1,2},{2,1},{5,6},{6,5},{9,10},{10,9},{13,14},{14,13},{17,18},{18,... | collective-permute-start | bytes 393224 | tf_op jit(solution)/shard_map/ppermute | solution.py:547
  41.7 21.6 %collective-permute-start.4 = (f32[15,64,128]{2,1,0:T(8,128)S(1)}, f32[15,64,128]{2,1,0:T(8,128)S(1)}, u32[]{:S(2)}, u32[]{:S(2)}) collective-permute-start(f32[15,64,128]{2,1,0:T(8,128)S(1)} %get-tuple-element.50.planes_a.refs_0_.refs_2_), channel_id=1, source_target_pairs={{0,4},{8,12},{16,20},{24,28},{4,0},{12,8},{20,16},{28,24},{1,5},{9... | collective-permute-start | bytes 1474568 | tf_op jit(solution)/shard_map/ppermute | solution.py:547
  42.3 21.0 %collective-permute-start.5 = (f32[15,64,128]{2,1,0:T(8,128)S(1)}, f32[15,64,128]{2,1,0:T(8,128)S(1)}, u32[]{:S(2)}, u32[]{:S(2)}) collective-permute-start(f32[15,64,128]{2,1,0:T(8,128)S(1)} %get-tuple-element.51.planes_b.refs_1_.refs_3_), channel_id=1, source_target_pairs={{4,8},{12,16},{20,24},{8,4},{16,12},{24,20},{5,9},{13,17},{21,25},... | collective-permute-start | bytes 1474568 | tf_op jit(solution)/shard_map/ppermute | solution.py:547
  45.9 1.4 %collective-permute-start.6 = (f32[256,128]{1,0:T(8,128)S(1)}, f32[256,128]{1,0:T(8,128)S(1)}, u32[]{:S(2)}, u32[]{:S(2)}) collective-permute-start(f32[256,128]{1,0:T(8,128)S(1)} %get-tuple-element.55), channel_id=1, source_target_pairs={{0,1},{2,3},{1,0},{3,2},{4,5},{6,7},{5,4},{7,6},{8,9},{10,11},{9,8... | collective-permute-start | bytes 393224 | tf_op jit(solution)/shard_map/ppermute | solution.py:547
  46.0 1.3 %collective-permute-start.7 = (f32[256,128]{1,0:T(8,128)S(1)}, f32[256,128]{1,0:T(8,128)S(1)}, u32[]{:S(2)}, u32[]{:S(2)}) collective-permute-start(f32[256,128]{1,0:T(8,128)S(1)} %get-tuple-element.56), channel_id=1, source_target_pairs={{1,2},{2,1},{5,6},{6,5},{9,10},{10,9},{13,14},{14,13},{17,18},{18,... | collective-permute-start | bytes 393224 | tf_op jit(solution)/shard_map/ppermute | solution.py:547
